TPU v7x, 128 devices: a whole 4x4x4 slice. The times are simulated.
128 devices in a mesh: grp: 8 (over x_lo, z), blk: 16 (over y, x_hi, core).
Axes of the slice: x: 4 (x_hi: 2, x_lo: 2; x = x_hi * 2 + x_lo), y: 4, z: 4, core: 2. Of those that a mesh axis runs over, the one named last changes fastest.
Arguments:
- pair_repr: bfloat16 [512, 512, 128], P(('grp', 'blk')), may hold values from -6 to 6
- pair_mask: int32 [512, 512], P(('grp', 'blk')), may hold values 0 or 1
- chain_index: int32 [512], replicated, may hold values from 0 to 3, never falling along the last dimension, each value on 1 to 256 neighbouring positions
- entity_embed: float32 [2, 128], replicated, may hold values from -3 to 3
- input_gain: float32 [2, 128], replicated, may hold values from 0.5 to 1.5
- input_bias: float32 [2, 128], replicated, may hold values from -2 to 2
- left_weight: bfloat16 [2, 128, 256], replicated, may hold values from -0.5 to 0.5
- right_weight: bfloat16 [2, 128, 256], replicated, may hold values from -0.5 to 0.5
- gate_weight: bfloat16 [2, 128, 128], replicated, may hold values from -0.5 to 0.5
- output_gain: float32 [2, 128], replicated, may hold values from 0.5 to 1.5
- output_bias: float32 [2, 128], replicated, may hold values from -2 to 2
- output_weight: bfloat16 [2, 128, 128], replicated, may hold values from -0.5 to 0.5
Outputs:
- pair_out: bfloat16 [512, 512, 128], P(('grp', 'blk'))
Inputs may be any that keep to these rules, and one draw needn't show every extreme that they name: `chain_index`: chain numbers never fall along the residues and every one of the 4 chains has at least one residue.
All inputs are finite; a program needn't handle non-finite values. No bound on the sum of `pair_mask` on one device may be relied on, other than what follows from the above.
Results may differ from a plain program's by a relative error of at most 0.0055.
Values may be sent and summed in bfloat16 or wider, within the bound.
A program may use at most 64 MiB of HBM per device.

v0:
```python
import jax
import jax.numpy as jnp
from jax import lax
from jax.sharding import PartitionSpec as P


def sent_together(arrays, axis, split_dim, concat_dim, along):
    widths = [a.shape[along] for a in arrays]
    both = jnp.concatenate(arrays, axis=along)
    whole = lax.all_to_all(both, axis, split_axis=split_dim, concat_axis=concat_dim, tiled=True)
    return tuple(jnp.split(whole, [sum(widths[:k]) for k in range(1, len(widths))], axis=along))


def normalize(values, gain_vector, bias_vector, along):
    average = jnp.mean(values, axis=along, keepdims=True)
    centered = values - average
    variance = jnp.mean(centered * centered, axis=along, keepdims=True)
    return centered * lax.rsqrt(variance + 1e-05) * gain_vector + bias_vector


def edge_values(normed, weight, mask_rows, hidden_count, row_count, columns):
    projected = lax.dot_general(
        weight, normed, (((0,), (1,)), ((), ())), preferred_element_type=jnp.float32
    )
    values = jax.nn.sigmoid(projected[:hidden_count]) * projected[hidden_count:] * mask_rows
    return values.astype(jnp.bfloat16).reshape(hidden_count, row_count, columns)


def to_planes(left_rows, right_rows, group_count, block_count):
    hidden_count, row_count, columns = left_rows.shape
    per_device = hidden_count // (group_count * block_count)
    shaped = (hidden_count, 1, row_count, columns)
    left_plane, right_plane = sent_together(
        (left_rows.reshape(shaped), right_rows.reshape(shaped)), ("grp", "blk"), 0, 1, 2
    )
    final = (per_device, group_count * block_count * row_count, columns)
    return (left_plane.reshape(final), right_plane.reshape(final))


def to_rows(product, group_count, block_count, row_count):
    per_device, total_rows, columns = product.shape
    shaped = product.reshape(1, per_device, group_count * block_count, row_count, columns)
    returned = lax.all_to_all(shaped, ("grp", "blk"), split_axis=2, concat_axis=0, tiled=True)
    return returned.reshape(-1, row_count * columns)


def shards(
    pair_repr,
    pair_mask,
    chain_index,
    entity_embed,
    input_gain,
    input_bias,
    left_weight,
    right_weight,
    gate_weight,
    output_gain,
    output_bias,
    output_weight,
):
    row_count, columns, channels = pair_repr.shape
    hidden_count = output_weight.shape[1]
    group_count = lax.axis_size("grp")
    block_count = lax.axis_size("blk")
    first_row = lax.axis_index(("grp", "blk")) * row_count
    own_chain = lax.dynamic_slice_in_dim(chain_index, first_row, row_count)
    same_chain = own_chain[:, None] == chain_index[None, :]
    current = pair_repr.astype(jnp.float32) + jnp.where(
        same_chain[:, :, None], entity_embed[1], entity_embed[0]
    )
    current = current.reshape(row_count * columns, channels)
    mask_rows = pair_mask.astype(jnp.float32).reshape(1, row_count * columns)
    contractions = [(((2,), (2,)), ((0,), (0,))), (((1,), (1,)), ((0,), (0,)))]
    stored = None
    for block_index in range(2):
        normed = normalize(current, input_gain[block_index], input_bias[block_index], 1).astype(
            jnp.bfloat16
        )
        left_rows = edge_values(
            normed, left_weight[block_index], mask_rows, hidden_count, row_count, columns
        )
        right_rows = edge_values(
            normed, right_weight[block_index], mask_rows, hidden_count, row_count, columns
        )
        gating = jax.nn.sigmoid(
            jnp.dot(normed, gate_weight[block_index], preferred_element_type=jnp.float32)
        )
        left_plane, right_plane = to_planes(left_rows, right_rows, group_count, block_count)
        product = lax.dot_general(
            left_plane, right_plane, contractions[block_index], preferred_element_type=jnp.float32
        ).astype(jnp.bfloat16)
        returned = to_rows(product, group_count, block_count, row_count).astype(jnp.float32)
        normed_out = normalize(
            returned, output_gain[block_index][:, None], output_bias[block_index][:, None], 0
        ).astype(jnp.bfloat16)
        update = lax.dot_general(
            normed_out,
            output_weight[block_index],
            (((0,), (0,)), ((), ())),
            preferred_element_type=jnp.float32,
        )
        stored = (current + gating * update).astype(jnp.bfloat16)
        current = lax.optimization_barrier(stored).astype(jnp.float32)
    return stored.reshape(row_count, columns, channels)


def solution(mesh):
    placed = (
        P(("grp", "blk"), None, None),
        P(("grp", "blk"), None),
        P(),
        P(),
        P(),
        P(),
        P(),
        P(),
        P(),
        P(),
        P(),
        P(),
    )
    return jax.shard_map(
        shards, mesh=mesh, in_specs=placed, out_specs=P(("grp", "blk"), None, None), check_vma=False
    )
```

profile of v0, /device:TPU:1, one launch (start us, length us, event | category | flops | bytes accessed | tf_op | source)
XLA Modules:
  0.0 113.2 jit_solution(7539058095854501350)
XLA Ops:
  0.0 0.8 dynamic_slice.3
  0.8 0.8 broadcast_compare_fusion
  1.5 0.8 slice_bitcast_fusion.13
  2.3 1.7 %fusion.49 = f32[4,512]{1,0:T(4,128)S(1)} fusion(f32[128]{0:T(128)S(1)} %get-tuple-element.22, f32[128]{0:T(128)S(1)} %get-tuple-element.21, pred[4,512]{1,0:T(4,128)(4,1)S(1)} %broadcast_compare_fusion, bf16[4,512,128]{2,1,0:T(8,128)(2,1)} %param.12), kind=kLoop, calls=%fused_computation.81 | loop fusion | flops 1046528 | bytes 535552 | tf_op jit(solution)/shard_map/reduce_sum | solution.py:15
  4.0 2.0 %multiply_reduce_fusion = f32[4,512]{1,0:T(4,128)S(1)} fusion(f32[4,512]{1,0:T(4,128)S(1)} %broadcast_multiply_fusion.3, f32[128]{0:T(128)S(1)} %get-tuple-element.22, f32[128]{0:T(128)S(1)} %get-tuple-element.21, pred[4,512]{1,0:T(4,128)(4,1)S(1)} %broadcast_compare_fusion, bf16[4,512,128]{2,1,0:T(8,128)(2,1)} %param.12), kind=kLoop, calls=%fused_computation.77 | loop fusion | flops 1570816 | bytes 543744 | tf_op jit(solution)/shard_map/reduce_sum | solution.py:17
  6.0 0.8 slice_bitcast_fusion.6
  6.8 2.0 %add_convert_fusion = (bf16[4,512,128]{2,1,0:T(8,128)(2,1)S(1)}, f32[4,512,128]{2,1,0:T(8,128)S(1)}) fusion(f32[128]{0:T(128)S(1)} %get-tuple-element.20, f32[128]{0:T(128)S(1)} %get-tuple-element.23, f32[4,512]{1,0:T(4,128)S(1)} %add_rsqrt_fusion.3, f32[4,512]{1,0:T(4,128)S(1)} %broadcast_multiply_fusion.3, f32[128]{0:T(128)S(1)} %get-tuple-element.22, ...), kind=kLoop, calls=%fused_computation.76 | loop fusion | flops 2097152 | bytes 2117632 | tf_op jit(solution)/shard_map/convert_element_type | solution.py:76
  8.8 0.4 convolution_bitcast_fusion.2
  9.2 0.4 convolution_bitcast_fusion.3
  9.7 0.6 fusion.45
  10.3 0.4 copy.21
  10.7 0.4 copy.22
  11.1 0.5 pad_maximum_fusion
  11.7 30.6 %all_to_all.42 = bf16[128,1,8,512]{3,2,1,0:T(8,128)(2,1)S(1)} all-to-all(bf16[128,1,8,512]{3,2,1,0:T(8,128)(2,1)S(1)} %pad_maximum_fusion), channel_id=1, replica_groups=mesh['grp'=8,'blk'=16] {'grp','blk'}, dimensions={0} | all-to-all | bytes 2097152 | tf_op jit(solution)/shard_map/all_to_all | solution.py:10
  42.3 0.3 fusion.69
  42.6 0.1 reshape.374
  42.7 0.1 reshape.375
  42.9 0.0 copy-start.4
  42.9 0.5 convolution_convert_fusion
  43.4 0.9 reshape.376
  44.3 4.1 %all-to-all-start.1 = ((bf16[1,1,128,4,512]{4,3,1,0,2:T(4,128)(2,1)}), bf16[1,1,128,4,512]{4,3,1,0,2:T(4,128)(2,1)S(1)}, u32[]{:S(2)}, u32[]{:S(2)}) async-start(bf16[1,1,128,4,512]{4,3,1,0,2:T(4,128)(2,1)} %bitcast.14), calls=%async_computation.1 | async-start | bytes 1048576 | tf_op jit(solution)/shard_map/all_to_all | solution.py:43
  48.4 1.2 %fusion.7 = f32[2048,128]{1,0:T(8,128)S(1)} fusion(bf16[2048,128]{1,0:T(8,128)(2,1)S(1)} %bitcast.95, bf16[2,128,128]{2,1,0:T(8,128)(2,1)} %param.20), kind=kOutput, calls=%fused_computation.15 | convolution fusion | flops 67895296 | bytes 1605632 | tf_op jit(solution)/shard_map/dot_general | solution.py:86
  49.6 12.6 %all-to-all-done.1 = bf16[1,1,128,4,512]{4,3,1,0,2:T(4,128)(2,1)S(1)} async-done(((bf16[1,1,128,4,512]{4,3,1,0,2:T(4,128)(2,1)}), bf16[1,1,128,4,512]{4,3,1,0,2:T(4,128)(2,1)S(1)}, u32[]{:S(2)}, u32[]{:S(2)}) %all-to-all-start.1) | async-done | bytes 524320 | tf_op jit(solution)/shard_map/all_to_all | solution.py:43
  62.2 0.3 convert_reduce_fusion.2
  62.5 0.4 fusion.21
  62.9 0.4 fusion.24
  63.3 0.1 copy.31
  63.4 0.3 fusion.8
  63.8 0.2 convert_reduce_fusion
  64.0 0.6 fusion.25
  64.7 0.7 convolution_bitcast_fusion
  65.4 0.7 convolution_bitcast_fusion.1
  66.1 0.6 fusion.35
  66.7 0.4 copy.24
  67.1 0.4 copy.25
  67.6 0.5 pad_maximum_fusion.1
  68.1 23.1 %all_to_all.43 = bf16[128,1,8,512]{3,2,1,0:T(8,128)(2,1)S(1)} all-to-all(bf16[128,1,8,512]{3,2,1,0:T(8,128)(2,1)S(1)} %pad_maximum_fusion.1), channel_id=1, replica_groups=mesh['grp'=8,'blk'=16] {'grp','blk'}, dimensions={0} | all-to-all | bytes 2097152 | tf_op jit(solution)/shard_map/all_to_all | solution.py:10
  91.2 0.3 copy.34
  91.5 0.5 fusion.10
  92.0 0.9 reshape.379
  92.9 4.1 %all-to-all-start.3 = ((bf16[1,1,128,4,512]{4,3,1,0,2:T(4,128)(2,1)}), bf16[1,1,128,4,512]{4,3,1,0,2:T(4,128)(2,1)S(1)}, u32[]{:S(2)}, u32[]{:S(2)}) async-start(bf16[1,1,128,4,512]{4,3,1,0,2:T(4,128)(2,1)} %bitcast.31), calls=%async_computation.3 | async-start | bytes 1048576 | tf_op jit(solution)/shard_map/all_to_all | solution.py:43
  97.0 0.7 fusion.3
  97.7 13.1 %all-to-all-done.3 = bf16[1,1,128,4,512]{4,3,1,0,2:T(4,128)(2,1)S(1)} async-done(((bf16[1,1,128,4,512]{4,3,1,0,2:T(4,128)(2,1)}), bf16[1,1,128,4,512]{4,3,1,0,2:T(4,128)(2,1)S(1)}, u32[]{:S(2)}, u32[]{:S(2)}) %all-to-all-start.3) | async-done | bytes 524320 | tf_op jit(solution)/shard_map/all_to_all | solution.py:43
  110.8 0.3 convert_reduce_fusion.1
  111.1 0.4 fusion.17
  111.5 0.4 fusion.20
  112.0 0.1 copy.32
  112.1 1.1 %fusion.9 = bf16[2048,128]{1,0:T(8,128)(2,1)} fusion(f32[2048,128]{1,0:T(8,128)S(1)} %fusion.3, bf16[128,2048]{1,0:T(8,128)(2,1)S(1)} %bitcast.105, bf16[2048,128]{1,0:T(8,128)(2,1)S(1)} %fusion.8, bf16[2,128,128]{2,1,0:T(8,128)(2,1)S(1)} %copy-done.2), kind=kOutput, calls=%fused_computation.17 | convolution fusion | flops 68157440 | bytes 2654208 | tf_op jit(solution)/shard_map/dot_general | solution.py:96
  (24 shorter events, 0.1 us)
Async XLA Ops:
  0.0 8.8 %copy-start = (bf16[2,128,256]{2,1,0:T(8,128)(2,1)S(1)}, bf16[2,128,256]{2,1,0:T(8,128)(2,1)}, u32[]{:S(2)}) copy-start(bf16[2,128,256]{2,1,0:T(8,128)(2,1)} %param.19) | copy-start | bytes 393220
  6.8 2.4 %copy-start.1 = (bf16[2,128,256]{2,1,0:T(8,128)(2,1)S(1)}, bf16[2,128,256]{2,1,0:T(8,128)(2,1)}, u32[]{:S(2)}) copy-start(bf16[2,128,256]{2,1,0:T(8,128)(2,1)} %param.18) | copy-start | bytes 393220
  8.8 0.9 copy-start.3
  42.9 5.5 %copy-start.4 = (f32[2,128]{1,0:T(2,128)S(1)}, f32[2,128]{1,0:T(2,128)}, u32[]{:S(2)}) copy-start(f32[2,128]{1,0:T(2,128)} %param.22) | copy-start | bytes 3076
  42.9 5.5 %copy-start.5 = (f32[2,128]{1,0:T(2,128)S(1)}, f32[2,128]{1,0:T(2,128)}, u32[]{:S(2)}) copy-start(f32[2,128]{1,0:T(2,128)} %param.21) | copy-start | bytes 3076
  44.3 17.9 %all-to-all-start.1 = ((bf16[1,1,128,4,512]{4,3,1,0,2:T(4,128)(2,1)}), bf16[1,1,128,4,512]{4,3,1,0,2:T(4,128)(2,1)S(1)}, u32[]{:S(2)}, u32[]{:S(2)}) async-start(bf16[1,1,128,4,512]{4,3,1,0,2:T(4,128)(2,1)} %bitcast.14), calls=%async_computation.1 | async-start | bytes 1048576 | tf_op jit(solution)/shard_map/all_to_all | solution.py:43
  49.6 13.9 %copy-start.2 = (bf16[2,128,128]{2,1,0:T(8,128)(2,1)S(1)}, bf16[2,128,128]{2,1,0:T(8,128)(2,1)}, u32[]{:S(2)}) copy-start(bf16[2,128,128]{2,1,0:T(8,128)(2,1)} %param.23) | copy-start | bytes 196612
  91.5 5.5 %copy-start.6 = (bf16[2,128,128]{2,1,0:T(8,128)(2,1)S(1)}, bf16[2,128,128]{2,1,0:T(8,128)(2,1)}, u32[]{:S(2)}) copy-start(bf16[2,128,128]{2,1,0:T(8,128)(2,1)} %param.20) | copy-start | bytes 196612
  92.9 17.9 %all-to-all-start.3 = ((bf16[1,1,128,4,512]{4,3,1,0,2:T(4,128)(2,1)}), bf16[1,1,128,4,512]{4,3,1,0,2:T(4,128)(2,1)S(1)}, u32[]{:S(2)}, u32[]{:S(2)}) async-start(bf16[1,1,128,4,512]{4,3,1,0,2:T(4,128)(2,1)} %bitcast.31), calls=%async_computation.3 | async-start | bytes 1048576 | tf_op jit(solution)/shard_map/all_to_all | solution.py:43
where the time goes:
time: 114 us; the launch traced here: 113 us
  blocking collectives  53.7 us (47%)
  waiting for transfers between devices  25.7 us (23%)
  other arithmetic  11.8 us (10%)
  starting transfers between devices  8.12 us (7%)
  local copies, waits for them, and re-layouts  6.95 us (6%)
  matrix products  6.63 us (6%)
    all_to_all x2, blocking collectives, sent_together(): lax.all_to_all(both, axis, split_axis=split_dim, concat_axis=concat_dim,...  53.7 us
    all_to_all x2, waiting for transfers between devices, to_rows(): lax.all_to_all(shaped, ('grp', 'blk'), split_axis=2, concat_axis=0, tiled...  25.7 us
    all_to_all x2, starting transfers between devices, to_rows(): lax.all_to_all(shaped, ('grp', 'blk'), split_axis=2, concat_axis=0, tiled...  8.12 us
    reduce_sum x4, other arithmetic, normalize(): variance = jnp.mean(centered * centered, axis=along, keepdims=True)  3.4 us
    reduce_sum x4, other arithmetic, normalize(): average = jnp.mean(values, axis=along, keepdims=True)  2.44 us
    dot_general x4, matrix products, edge_values(): lax.dot_general(weight, normed, (((0,), (1,)), ((), ())), preferred_eleme...  2.31 us
  transfers between devices with their start and end apart: 2, of which 2 were waited for; matrix products, arithmetic and copies ran while one was open for 2% of the time, Pallas kernels for 0%

commit v1 on v0

v1 whole, which is shorter than its diff:
```python
import jax
import jax.numpy as jnp
from jax import lax
from jax.experimental import pallas as pl
from jax.experimental.pallas import tpu as pltpu
from jax.sharding import PartitionSpec as P

F32, BF16 = jnp.float32, jnp.bfloat16
MESH = pl.DeviceIdType.MESH
LANES = 128
CHUNKS = 2
NN, NT = ((1,), (0,)), ((1,), (1,))


def dot(a, b, dims):
    return lax.dot_general(a, b, (dims, ((), ())), preferred_element_type=F32)


def layer_norm(values, gain, bias):
    average = jnp.mean(values, axis=0, keepdims=True)
    centered = values - average
    variance = jnp.mean(centered * centered, axis=0, keepdims=True)
    return (centered * lax.rsqrt(variance + 1e-05) * gain + bias).astype(BF16)


def body(
    x_ref,
    mask_ref,
    own_chain_ref,
    chain_ref,
    embed_ref,
    in_gain_ref,
    in_bias_ref,
    left_ref,
    right_ref,
    gate_ref,
    out_gain_ref,
    out_bias_ref,
    out_w_ref,
    out_ref,
    cols,
    w_in,
    w_out,
    state,
    gating,
    mask_rows,
    spread,
    left_t,
    edge_send,
    edge_recv,
    prod_send,
    prod_recv,
    edge_ssem,
    edge_rsem,
    prod_ssem,
    prod_rsem,
    own_sem,
):
    rows, columns, chan = x_ref.shape
    blocks = columns // LANES
    wide = rows * LANES
    per = blocks // CHUNKS
    blk_count = lax.axis_size("blk")
    devices = lax.axis_size("grp") * blk_count
    plane = devices * rows
    me = lax.axis_index("grp") * blk_count + lax.axis_index("blk")

    def place(index):
        return (index // blk_count, lax.rem(index, blk_count))

    barrier = pltpu.get_barrier_semaphore()

    def greet(step, carry):
        pl.semaphore_signal(
            barrier, inc=1, device_id=place(lax.rem(me + step, devices)), device_id_type=MESH
        )
        return carry

    lax.fori_loop(1, devices, greet, 0)

    eye = (
        lax.broadcasted_iota(jnp.int32, (LANES, LANES), 0)
        == lax.broadcasted_iota(jnp.int32, (LANES, LANES), 1)
    ).astype(BF16)

    def column(vector):
        return jnp.transpose(jnp.broadcast_to(vector, (LANES, chan)))

    def four(block):
        return jnp.concatenate([block] * rows, axis=1)

    def prepare(u):
        for k, ref in enumerate((in_gain_ref, in_bias_ref, out_gain_ref, out_bias_ref)):
            cols[4 * u + k] = column(ref[u : u + 1, :])
        for k in range(2):
            w_in[u, k * LANES : (k + 1) * LANES, :] = jnp.transpose(
                left_ref[u, :, k * LANES : (k + 1) * LANES]
            )
            w_in[u, (2 + k) * LANES : (3 + k) * LANES, :] = jnp.transpose(
                right_ref[u, :, k * LANES : (k + 1) * LANES]
            )
        w_in[u, 4 * LANES :, :] = jnp.transpose(gate_ref[u])
        w_out[u] = jnp.transpose(out_w_ref[u])

    def load(cb):
        span = slice(cb * LANES, (cb + 1) * LANES)
        other, same = cols[8], cols[9]
        parts, masks = [], []
        for r in range(rows):
            flat = dot(eye, x_ref[r, span, :], NT)
            together = chain_ref[cb : cb + 1, :] == own_chain_ref[me * rows + r]
            parts.append(flat + jnp.where(together, same, other))
            masks.append(mask_ref[r : r + 1, span].astype(F32))
        state[cb] = jnp.concatenate(parts, axis=1)
        mask_rows[cb] = jnp.concatenate(masks, axis=1)

    def edges(u, cb):
        normed = layer_norm(state[cb], four(cols[4 * u]), four(cols[4 * u + 1]))
        for side in range(2):
            low = side * 2 * LANES
            gate = dot(w_in[u, low : low + LANES, :], normed, NN)
            value = dot(w_in[u, low + LANES : low + 2 * LANES, :], normed, NN)
            value = jax.nn.sigmoid(gate) * value * mask_rows[cb]
            for r in range(rows):
                spread[side, pl.ds(r, LANES, stride=rows), :] = value[:, r * LANES : (r + 1) * LANES]
            edge_send.at[u, cb, side].reshape(LANES * rows, LANES)[...] = spread[side].astype(BF16)
        gating[cb] = jax.nn.sigmoid(dot(w_in[u, 4 * LANES :, :], normed, NN))

    def finish(u, cb):
        spread[0] = prod_recv.at[u, cb].reshape(LANES * rows, LANES)[...].astype(F32)
        product = jnp.concatenate(
            [spread[0, pl.ds(r, LANES, stride=rows), :] for r in range(rows)], axis=1
        )
        normed = layer_norm(product, four(cols[4 * u + 2]), four(cols[4 * u + 3]))
        update = dot(w_out[u], normed, NN)
        new = (state[cb] + gating[cb] * update).astype(BF16)
        if u == 0:
            state[cb] = new.astype(F32)
        else:
            for r in range(rows):
                out_ref[r, cb * LANES : (cb + 1) * LANES, :] = dot(
                    eye, new[:, r * LANES : (r + 1) * LANES], NT
                ).astype(BF16)

    def edge_parts(u, ch, source, target):
        span = pl.ds(ch * per, per)
        return edge_send.at[u, span, :, source], edge_recv.at[u, span, :, target]

    def prod_parts(u, ch, source, target):
        span = pl.ds(ch * per, per)
        return prod_send.at[u, span, source], prod_recv.at[u, span, target]

    def send_all(parts, u, ch, ssem, rsem):
        def send(step, carry):
            to = lax.rem(me + step, devices)
            source, target = parts(u, ch, to, me)
            pltpu.make_async_remote_copy(
                src_ref=source,
                dst_ref=target,
                send_sem=ssem.at[u, ch],
                recv_sem=rsem.at[u, ch],
                device_id=place(to),
                device_id_type=MESH,
            ).start()
            return carry

        lax.fori_loop(1, devices, send, 0)
        source, target = parts(u, ch, me, me)
        own = pltpu.make_async_copy(source, target, own_sem)
        own.start()
        own.wait()

    def arrival(parts, u, ch, ssem, rsem):
        source, target = parts(u, ch, pl.ds(0, devices - 1), pl.ds(0, devices - 1))
        return pltpu.make_async_remote_copy(
            src_ref=source,
            dst_ref=target,
            send_sem=ssem.at[u, ch],
            recv_sem=rsem.at[u, ch],
            device_id=place(me),
            device_id_type=MESH,
        )

    def plane_of(u, cb, side):
        return edge_recv.at[u, cb, side].reshape(plane, LANES)

    edge_args = (edge_parts,)
    for k in range(2):
        cols[8 + k] = column(embed_ref[k : k + 1, :])
    prepare(0)
    for ch in range(CHUNKS):
        for cb in range(ch * per, (ch + 1) * per):
            load(cb)
            edges(0, cb)
        if ch == 0:
            pl.semaphore_wait(barrier, devices - 1)
        send_all(edge_parts, 0, ch, edge_ssem, edge_rsem)
    prepare(1)

    for u in range(2):
        if u == 0:
            for ch in range(CHUNKS):
                arrival(edge_parts, u, ch, edge_ssem, edge_rsem).wait_recv()
            left = jnp.concatenate([plane_of(0, cb, 0)[...] for cb in range(blocks)], axis=1)
        else:
            for ch in range(CHUNKS):
                arrival(edge_parts, u, ch, edge_ssem, edge_rsem).wait_recv()
                for cb in range(ch * per, (ch + 1) * per):
                    left_t[cb * LANES : (cb + 1) * LANES, :] = jnp.transpose(plane_of(1, cb, 0)[...])
            left = left_t[...]
        for ch in range(CHUNKS):
            for jb in range(ch * per, (ch + 1) * per):
                if u == 0:
                    right = jnp.concatenate(
                        [
                            plane_of(0, cb, 1)[jb * LANES : (jb + 1) * LANES, :]
                            for cb in range(blocks)
                        ],
                        axis=1,
                    )
                    product = dot(left, right, NT)
                else:
                    product = dot(left, plane_of(1, jb, 1)[...], NN)
                prod_send.at[u, jb].reshape(plane, LANES)[...] = product.astype(BF16)
            send_all(prod_parts, u, ch, prod_ssem, prod_rsem)
        for ch in range(CHUNKS):
            arrival(prod_parts, u, ch, prod_ssem, prod_rsem).wait_recv()
            for cb in range(ch * per, (ch + 1) * per):
                finish(u, cb)
                if u == 0:
                    edges(1, cb)
            if u == 0:
                send_all(edge_parts, 1, ch, edge_ssem, edge_rsem)
    for u in range(2):
        for ch in range(CHUNKS):
            arrival(edge_parts, u, ch, edge_ssem, edge_rsem).wait_send()
            arrival(prod_parts, u, ch, prod_ssem, prod_rsem).wait_send()


def shards(
    pair_repr,
    pair_mask,
    chain_index,
    entity_embed,
    input_gain,
    input_bias,
    left_weight,
    right_weight,
    gate_weight,
    output_gain,
    output_bias,
    output_weight,
):
    rows, columns, chan = pair_repr.shape
    devices = lax.axis_size("grp") * lax.axis_size("blk")
    blocks = columns // LANES
    wide = rows * LANES
    vmem = pl.BlockSpec(memory_space=pltpu.VMEM)
    specs = [vmem, vmem, pl.BlockSpec(memory_space=pltpu.SMEM)] + [vmem] * 10
    return pl.pallas_call(
        body,
        out_shape=jax.ShapeDtypeStruct((rows, columns, chan), BF16),
        in_specs=specs,
        out_specs=vmem,
        scratch_shapes=[
            pltpu.VMEM((10, LANES, LANES), F32),
            pltpu.VMEM((2, 5 * LANES, chan), BF16),
            pltpu.VMEM((2, LANES, LANES), BF16),
            pltpu.VMEM((blocks, chan, wide), F32),
            pltpu.VMEM((blocks, chan, wide), F32),
            pltpu.VMEM((blocks, 1, wide), F32),
            pltpu.VMEM((2, LANES * rows, LANES), F32),
            pltpu.VMEM((columns, devices * rows), BF16),
            pltpu.VMEM((2, blocks, 2, LANES, rows, LANES), BF16),
            pltpu.VMEM((2, blocks, 2, devices, rows, LANES), BF16),
            pltpu.VMEM((2, blocks, devices, rows, LANES), BF16),
            pltpu.VMEM((2, blocks, LANES, rows, LANES), BF16),
            pltpu.SemaphoreType.DMA((2, CHUNKS)),
            pltpu.SemaphoreType.DMA((2, CHUNKS)),
            pltpu.SemaphoreType.DMA((2, CHUNKS)),
            pltpu.SemaphoreType.DMA((2, CHUNKS)),
            pltpu.SemaphoreType.DMA,
        ],
        compiler_params=pltpu.CompilerParams(
            collective_id=0, has_side_effects=True, vmem_limit_bytes=40 * 1024 * 1024
        ),
        name="triangle_updates",
    )(
        pair_repr,
        pair_mask,
        chain_index,
        chain_index.reshape(blocks, LANES),
        entity_embed,
        input_gain,
        input_bias,
        left_weight,
        right_weight,
        gate_weight,
        output_gain,
        output_bias,
        output_weight,
    )


def solution(mesh):
    rows = P(("grp", "blk"), None, None)
    placed = (rows, P(("grp", "blk"), None)) + (P(),) * 10
    return jax.shard_map(shards, mesh=mesh, in_specs=placed, out_specs=rows, check_vma=False)
```

time: 114 us -> 76.6 us (0.67)
  Pallas kernels: 0 us -> 66 us
  blocking collectives: 53.7 us -> 0 us
  waiting for transfers between devices: 25.7 us -> 0 us
  other arithmetic: 11.8 us -> 0 us
  starting transfers between devices: 8.12 us -> 0 us
  matrix products: 6.63 us -> 0 us
  local copies, waits for them, and re-layouts: 6.95 us -> 10.1 us
    pallas_call x0 -> x1, Pallas kernels: none -> 66 us  [shards(): pl.pallas_call(body, out_shape=jax.ShapeDtypeStruct((rows, columns, chan)...]
    all_to_all x2 -> x0, blocking collectives: 53.7 us -> none  [sent_together(): lax.all_to_all(both, axis, split_axis=split_dim, concat_axis=concat_dim,...]
    all_to_all x2 -> x0, waiting for transfers between devices: 25.7 us -> none  [to_rows(): lax.all_to_all(shaped, ('grp', 'blk'), split_axis=2, concat_axis=0, tiled...]
    unnamed x17 -> x25, local copies, waits for them, and re-layouts: 0.25 us -> 10.1 us
    all_to_all x2 -> x0, starting transfers between devices: 8.12 us -> none  [to_rows(): lax.all_to_all(shaped, ('grp', 'blk'), split_axis=2, concat_axis=0, tiled...]
    dot_general x10 -> x0, matrix products: 6.63 us -> none  [the longest x4 2.31 us: edge_values(): lax.dot_general(weight, normed, (((0,), (1,)), ((), ())), preferred_eleme...]
    reduce_sum x8 -> x0, other arithmetic: 5.84 us -> none  [the longest x4 3.4 us: normalize(): variance = jnp.mean(centered * centered, axis=along, keepdims=True)]
    convert_element_type x5 -> x0, other arithmetic: 4.02 us -> none  [the longest x1 1.99 us: shards(): normalize(current, input_gain[block_index], input_bias[block_index], 1)]
  transfers between devices with their start and end apart: 2 -> 0, of which waited for: 2 -> 0; matrix products, arithmetic and copies ran while one was open for 2% -> 0% of each run, Pallas kernels for 0% -> 0%
where the time goes in v1:
time: 76.6 us; the launch traced here: 76.2 us
  Pallas kernels  66 us (86%)
  local copies, waits for them, and re-layouts  10.1 us (13%)
    pallas_call x1, Pallas kernels, shards(): pl.pallas_call(body, out_shape=jax.ShapeDtypeStruct((rows, columns, chan)...  66 us
    unnamed x25, local copies, waits for them, and re-layouts  10.1 us

profile of v1, /device:TPU:1, one launch (start us, length us, event | category | flops | bytes accessed | tf_op | source)
XLA Modules:
  0.0 76.2 jit_solution(13355316765803084742)
XLA Ops:
  0.0 0.0 copy-start.7
  0.0 0.7 copy-done.7
  0.7 0.0 copy-start
  0.7 1.0 %copy-done = bf16[4,512,128]{2,1,0:T(8,128)(2,1)S(1)} copy-done((bf16[4,512,128]{2,1,0:T(8,128)(2,1)S(1)}, bf16[4,512,128]{2,1,0:T(8,128)(2,1)}, u32[]{:S(2)}) %copy-start) | copy-done | bytes 524312
  1.7 0.0 copy-start.1
  1.7 0.9 %copy-done.1 = bf16[2,128,256]{2,1,0:T(8,128)(2,1)S(1)} copy-done((bf16[2,128,256]{2,1,0:T(8,128)(2,1)S(1)}, bf16[2,128,256]{2,1,0:T(8,128)(2,1)}, u32[]{:S(2)}) %copy-start.1) | copy-done | bytes 131096
  2.6 0.0 copy-start.2
  2.6 0.9 %copy-done.2 = bf16[2,128,256]{2,1,0:T(8,128)(2,1)S(1)} copy-done((bf16[2,128,256]{2,1,0:T(8,128)(2,1)S(1)}, bf16[2,128,256]{2,1,0:T(8,128)(2,1)}, u32[]{:S(2)}) %copy-start.2) | copy-done | bytes 131096
  3.5 0.0 copy-start.3
  3.5 0.8 %copy-done.3 = bf16[2,128,128]{2,1,0:T(8,128)(2,1)S(1)} copy-done((bf16[2,128,128]{2,1,0:T(8,128)(2,1)S(1)}, bf16[2,128,128]{2,1,0:T(8,128)(2,1)}, u32[]{:S(2)}) %copy-start.3) | copy-done | bytes 65560
  4.4 0.0 copy-start.4
  4.4 0.8 %copy-done.4 = bf16[2,128,128]{2,1,0:T(8,128)(2,1)S(1)} copy-done((bf16[2,128,128]{2,1,0:T(8,128)(2,1)S(1)}, bf16[2,128,128]{2,1,0:T(8,128)(2,1)}, u32[]{:S(2)}) %copy-start.4) | copy-done | bytes 65560
  5.2 0.0 copy-start.5
  5.2 0.7 copy-done.5
  5.9 0.0 copy-start.6
  5.9 0.7 copy-done.6
  6.6 0.0 copy-start.8
  6.6 0.7 copy-done.8
  7.3 0.0 copy-start.9
  7.3 0.7 copy-done.9
  8.0 0.0 copy-start.10
  8.0 0.7 copy-done.10
  8.6 0.0 copy-start.11
  8.6 0.7 copy-done.11
  9.3 66.0 %triangle_updates.1 = bf16[4,512,128]{2,1,0:T(8,128)(2,1)S(1)} custom-call(bf16[4,512,128]{2,1,0:T(8,128)(2,1)S(1)} %copy-done, s32[4,512]{1,0:T(4,128)S(1)} %copy-done.5, s32[512]{0:T(512)S(1)} %copy-done.6, s32[4,128]{1,0:T(4,128)S(1)} %bitcast.1, f32[2,128]{1,0:T(2,128)S(1)} %copy-done.7, f32[2,128]{1,0:T(2,128)S(1)} %copy-done.8, ...), custom_call_target="tpu_custom_call" | custom-call | tf_op jit(solution)/shard_map/triangle_updates/pallas_call | solution.py:260
  75.4 0.8 %copy.14 = bf16[4,512,128]{2,1,0:T(8,128)(2,1)} copy(bf16[4,512,128]{2,1,0:T(8,128)(2,1)S(1)} %triangle_updates.1) | data formatting | bytes 1048576
Async XLA Ops:
  0.0 0.7 copy-start.7
  0.7 1.0 %copy-start = (bf16[4,512,128]{2,1,0:T(8,128)(2,1)S(1)}, bf16[4,512,128]{2,1,0:T(8,128)(2,1)}, u32[]{:S(2)}) copy-start(bf16[4,512,128]{2,1,0:T(8,128)(2,1)} %x_ref.1) | copy-start | bytes 1572868
  1.7 0.9 %copy-start.1 = (bf16[2,128,256]{2,1,0:T(8,128)(2,1)S(1)}, bf16[2,128,256]{2,1,0:T(8,128)(2,1)}, u32[]{:S(2)}) copy-start(bf16[2,128,256]{2,1,0:T(8,128)(2,1)} %left_ref.1) | copy-start | bytes 393220
  2.6 0.9 %copy-start.2 = (bf16[2,128,256]{2,1,0:T(8,128)(2,1)S(1)}, bf16[2,128,256]{2,1,0:T(8,128)(2,1)}, u32[]{:S(2)}) copy-start(bf16[2,128,256]{2,1,0:T(8,128)(2,1)} %right_ref.1) | copy-start | bytes 393220
  3.5 0.8 %copy-start.3 = (bf16[2,128,128]{2,1,0:T(8,128)(2,1)S(1)}, bf16[2,128,128]{2,1,0:T(8,128)(2,1)}, u32[]{:S(2)}) copy-start(bf16[2,128,128]{2,1,0:T(8,128)(2,1)} %gate_ref.1) | copy-start | bytes 196612
  4.4 0.8 %copy-start.4 = (bf16[2,128,128]{2,1,0:T(8,128)(2,1)S(1)}, bf16[2,128,128]{2,1,0:T(8,128)(2,1)}, u32[]{:S(2)}) copy-start(bf16[2,128,128]{2,1,0:T(8,128)(2,1)} %out_w_ref.1) | copy-start | bytes 196612
  5.2 0.7 copy-start.5
  5.9 0.7 copy-start.6
  6.6 0.7 copy-start.8
  7.3 0.7 copy-start.9
  8.0 0.7 copy-start.10
  8.6 0.7 copy-start.11

commit v2 on v1

--- a/solution.py
+++ b/solution.py
@@ -24,9 +24,21 @@
 
 
 def body(
+    x_hbm,
+    mask_hbm,
+    chain_hbm,
+    embed_hbm,
+    in_gain_hbm,
+    in_bias_hbm,
+    left_hbm,
+    right_hbm,
+    gate_hbm,
+    out_gain_hbm,
+    out_bias_hbm,
+    out_w_hbm,
+    out_ref,
     x_ref,
     mask_ref,
-    own_chain_ref,
     chain_ref,
     embed_ref,
     in_gain_ref,
@@ -37,7 +49,8 @@
     out_gain_ref,
     out_bias_ref,
     out_w_ref,
-    out_ref,
+    own_chain_ref,
+    in_sems,
     cols,
     w_in,
     w_out,
@@ -56,9 +69,8 @@
     prod_rsem,
     own_sem,
 ):
-    rows, columns, chan = x_ref.shape
+    rows, columns, chan = x_hbm.shape
     blocks = columns // LANES
-    wide = rows * LANES
     per = blocks // CHUNKS
     blk_count = lax.axis_size("blk")
     devices = lax.axis_size("grp") * blk_count
@@ -68,6 +80,30 @@
     def place(index):
         return (index // blk_count, lax.rem(index, blk_count))
 
+    loads = {}
+
+    def fetch(name, source, target):
+        loads[name] = pltpu.make_async_copy(source, target, in_sems.at[len(loads)])
+        loads[name].start()
+
+    def fetched(*wanted):
+        for name in wanted:
+            loads[name].wait()
+
+    fetch("embed", embed_hbm, embed_ref)
+    fetch("in_gain", in_gain_hbm, in_gain_ref)
+    fetch("in_bias", in_bias_hbm, in_bias_ref)
+    fetch("left", left_hbm, left_ref)
+    fetch("right", right_hbm, right_ref)
+    fetch("gate", gate_hbm, gate_ref)
+    fetch("x", x_hbm, x_ref)
+    fetch("chain", chain_hbm, chain_ref)
+    fetch("own_chain", chain_hbm, own_chain_ref)
+    fetch("mask", mask_hbm, mask_ref)
+    fetch("out_gain", out_gain_hbm, out_gain_ref)
+    fetch("out_bias", out_bias_hbm, out_bias_ref)
+    fetch("out_w", out_w_hbm, out_w_ref)
+
     barrier = pltpu.get_barrier_semaphore()
 
     def greet(step, carry):
@@ -89,9 +125,14 @@
     def four(block):
         return jnp.concatenate([block] * rows, axis=1)
 
-    def prepare(u):
-        for k, ref in enumerate((in_gain_ref, in_bias_ref, out_gain_ref, out_bias_ref)):
-            cols[4 * u + k] = column(ref[u : u + 1, :])
+    def prepare_out(u):
+        cols[4 * u + 2] = column(out_gain_ref[u : u + 1, :])
+        cols[4 * u + 3] = column(out_bias_ref[u : u + 1, :])
+        w_out[u] = jnp.transpose(out_w_ref[u])
+
+    def prepare_in(u):
+        cols[4 * u] = column(in_gain_ref[u : u + 1, :])
+        cols[4 * u + 1] = column(in_bias_ref[u : u + 1, :])
         for k in range(2):
             w_in[u, k * LANES : (k + 1) * LANES, :] = jnp.transpose(
                 left_ref[u, :, k * LANES : (k + 1) * LANES]
@@ -100,7 +141,6 @@
                 right_ref[u, :, k * LANES : (k + 1) * LANES]
             )
         w_in[u, 4 * LANES :, :] = jnp.transpose(gate_ref[u])
-        w_out[u] = jnp.transpose(out_w_ref[u])
 
     def load(cb):
         span = slice(cb * LANES, (cb + 1) * LANES)
@@ -108,7 +148,7 @@
         parts, masks = [], []
         for r in range(rows):
             flat = dot(eye, x_ref[r, span, :], NT)
-            together = chain_ref[cb : cb + 1, :] == own_chain_ref[me * rows + r]
+            together = chain_ref[pl.ds(cb * LANES, LANES)][None, :] == own_chain_ref[me * rows + r]
             parts.append(flat + jnp.where(together, same, other))
             masks.append(mask_ref[r : r + 1, span].astype(F32))
         state[cb] = jnp.concatenate(parts, axis=1)
@@ -184,10 +224,11 @@
     def plane_of(u, cb, side):
         return edge_recv.at[u, cb, side].reshape(plane, LANES)
 
-    edge_args = (edge_parts,)
+    fetched("embed", "in_gain", "in_bias", "left", "right", "gate")
     for k in range(2):
         cols[8 + k] = column(embed_ref[k : k + 1, :])
-    prepare(0)
+    prepare_in(0)
+    fetched("x", "chain", "own_chain", "mask")
     for ch in range(CHUNKS):
         for cb in range(ch * per, (ch + 1) * per):
             load(cb)
@@ -195,7 +236,10 @@
         if ch == 0:
             pl.semaphore_wait(barrier, devices - 1)
         send_all(edge_parts, 0, ch, edge_ssem, edge_rsem)
-    prepare(1)
+    fetched("out_gain", "out_bias", "out_w")
+    prepare_out(0)
+    prepare_in(1)
+    prepare_out(1)
 
     for u in range(2):
         if u == 0:
@@ -255,14 +299,29 @@
     devices = lax.axis_size("grp") * lax.axis_size("blk")
     blocks = columns // LANES
     wide = rows * LANES
-    vmem = pl.BlockSpec(memory_space=pltpu.VMEM)
-    specs = [vmem, vmem, pl.BlockSpec(memory_space=pltpu.SMEM)] + [vmem] * 10
+    arguments = (
+        pair_repr,
+        pair_mask,
+        chain_index,
+        entity_embed,
+        input_gain,
+        input_bias,
+        left_weight,
+        right_weight,
+        gate_weight,
+        output_gain,
+        output_bias,
+        output_weight,
+    )
     return pl.pallas_call(
         body,
         out_shape=jax.ShapeDtypeStruct((rows, columns, chan), BF16),
-        in_specs=specs,
-        out_specs=vmem,
-        scratch_shapes=[
+        in_specs=[pl.BlockSpec(memory_space=pltpu.HBM)] * len(arguments),
+        out_specs=pl.BlockSpec(memory_space=pltpu.VMEM),
+        scratch_shapes=[pltpu.VMEM(a.shape, a.dtype) for a in arguments]
+        + [
+            pltpu.SMEM(chain_index.shape, chain_index.dtype),
+            pltpu.SemaphoreType.DMA((len(arguments) + 1,)),
             pltpu.VMEM((10, LANES, LANES), F32),
             pltpu.VMEM((2, 5 * LANES, chan), BF16),
             pltpu.VMEM((2, LANES, LANES), BF16),
@@ -285,21 +344,7 @@
             collective_id=0, has_side_effects=True, vmem_limit_bytes=40 * 1024 * 1024
         ),
         name="triangle_updates",
-    )(
-        pair_repr,
-        pair_mask,
-        chain_index,
-        chain_index.reshape(blocks, LANES),
-        entity_embed,
-        input_gain,
-        input_bias,
-        left_weight,
-        right_weight,
-        gate_weight,
-        output_gain,
-        output_bias,
-        output_weight,
-    )
+    )(*[pltpu.with_memory_space_constraint(a, pltpu.HBM) for a in arguments])
 
 
 def solution(mesh):

time: 76.6 us -> 66.4 us (0.87)
  local copies, waits for them, and re-layouts: 10.1 us -> 0.8 us
    unnamed x25 -> x1, local copies, waits for them, and re-layouts: 10.1 us -> 0.8 us
where the time goes in v2:
time: 66.4 us; the launch traced here: 66.3 us
  Pallas kernels  65.5 us (99%)
  local copies, waits for them, and re-layouts  0.8 us (1%)
    pallas_call x1, Pallas kernels, shards(): pl.pallas_call(body, out_shape=jax.ShapeDtypeStruct((rows, columns, chan)...  65.5 us

profile of v2, /device:TPU:1, one launch (start us, length us, event | category | flops | bytes accessed | tf_op | source)
XLA Modules:
  0.0 66.3 jit_solution(7532791657126881022)
XLA Ops:
  0.0 65.5 %triangle_updates.1 = bf16[4,512,128]{2,1,0:T(8,128)(2,1)S(1)} custom-call(bf16[4,512,128]{2,1,0:T(8,128)(2,1)} %x_hbm.1, s32[4,512]{1,0:T(4,128)} %mask_hbm.1, s32[512]{0:T(512)} %chain_hbm.1, f32[2,128]{1,0:T(2,128)} %embed_hbm.1, f32[2,128]{1,0:T(2,128)} %in_gain_hbm.1, f32[2,128]{1,0:T(2,128)} %in_bias_hbm.1, bf16[2,128,256]{2,1,0:T(8,128)(2,1)} %left_hbm.1, ...), custom_call_target="tpu_custom_call" | custom-call | tf_op jit(solution)/shard_map/triangle_updates/pallas_call | solution.py:316
  65.5 0.8 %copy.14 = bf16[4,512,128]{2,1,0:T(8,128)(2,1)} copy(bf16[4,512,128]{2,1,0:T(8,128)(2,1)S(1)} %triangle_updates.1) | data formatting | bytes 1048576

commit v3 on v2

--- a/solution.py
+++ b/solution.py
@@ -6,9 +6,12 @@
 from jax.sharding import PartitionSpec as P
 
 F32, BF16 = jnp.float32, jnp.bfloat16
-MESH = pl.DeviceIdType.MESH
+LOGICAL = pl.DeviceIdType.LOGICAL
 LANES = 128
-CHUNKS = 2
+EDGE_PARTS = (((0, 4), (4, 8)), ((0, 2), (2, 4), (4, 6), (6, 7), (7, 8)))
+PROD_PARTS = (((0, 1), (1, 2), (2, 3), (3, 4)), ((0, 1), (1, 2), (2, 3), (3, 4)))
+MOST = 5
+UNROLL = 8
 NN, NT = ((1,), (0,)), ((1,), (1,))
 
 
@@ -56,6 +59,7 @@
     w_out,
     state,
     gating,
+    normed_rows,
     mask_rows,
     spread,
     left_t,
@@ -67,18 +71,15 @@
     edge_rsem,
     prod_ssem,
     prod_rsem,
-    own_sem,
+    edge_own,
+    prod_own,
 ):
     rows, columns, chan = x_hbm.shape
     blocks = columns // LANES
-    per = blocks // CHUNKS
     blk_count = lax.axis_size("blk")
     devices = lax.axis_size("grp") * blk_count
     plane = devices * rows
     me = lax.axis_index("grp") * blk_count + lax.axis_index("blk")
-
-    def place(index):
-        return (index // blk_count, lax.rem(index, blk_count))
 
     loads = {}
 
@@ -108,11 +109,11 @@
 
     def greet(step, carry):
         pl.semaphore_signal(
-            barrier, inc=1, device_id=place(lax.rem(me + step, devices)), device_id_type=MESH
+            barrier, inc=1, device_id=lax.rem(me + step, devices), device_id_type=LOGICAL
         )
         return carry
 
-    lax.fori_loop(1, devices, greet, 0)
+    lax.fori_loop(1, devices, greet, 0, unroll=UNROLL)
 
     eye = (
         lax.broadcasted_iota(jnp.int32, (LANES, LANES), 0)
@@ -156,6 +157,7 @@
 
     def edges(u, cb):
         normed = layer_norm(state[cb], four(cols[4 * u]), four(cols[4 * u + 1]))
+        normed_rows[cb] = normed
         for side in range(2):
             low = side * 2 * LANES
             gate = dot(w_in[u, low : low + LANES, :], normed, NN)
@@ -163,8 +165,10 @@
             value = jax.nn.sigmoid(gate) * value * mask_rows[cb]
             for r in range(rows):
                 spread[side, pl.ds(r, LANES, stride=rows), :] = value[:, r * LANES : (r + 1) * LANES]
-            edge_send.at[u, cb, side].reshape(LANES * rows, LANES)[...] = spread[side].astype(BF16)
-        gating[cb] = jax.nn.sigmoid(dot(w_in[u, 4 * LANES :, :], normed, NN))
+            edge_send.at[u, 2 * cb + side].reshape(LANES * rows, LANES)[...] = spread[side].astype(BF16)
+
+    def gate(u, cb):
+        gating[cb] = jax.nn.sigmoid(dot(w_in[u, 4 * LANES :, :], normed_rows[cb], NN))
 
     def finish(u, cb):
         spread[0] = prod_recv.at[u, cb].reshape(LANES * rows, LANES)[...].astype(F32)
@@ -182,103 +186,123 @@
                     eye, new[:, r * LANES : (r + 1) * LANES], NT
                 ).astype(BF16)
 
-    def edge_parts(u, ch, source, target):
-        span = pl.ds(ch * per, per)
-        return edge_send.at[u, span, :, source], edge_recv.at[u, span, :, target]
-
-    def prod_parts(u, ch, source, target):
-        span = pl.ds(ch * per, per)
-        return prod_send.at[u, span, source], prod_recv.at[u, span, target]
-
-    def send_all(parts, u, ch, ssem, rsem):
+    edge_stage = (EDGE_PARTS, edge_send, edge_recv, edge_ssem, edge_rsem, edge_own)
+    prod_stage = (PROD_PARTS, prod_send, prod_recv, prod_ssem, prod_rsem, prod_own)
+
+    def ends(stage, u, part, source, target):
+        parts, sent, received = stage[:3]
+        low, high = parts[u][part]
+        span = pl.ds(low, high - low)
+        return sent.at[u, span, source], received.at[u, span, target]
+
+    def send_all(stage, u, part):
+        ssem, rsem, own_sem = stage[3:]
+        source, target = ends(stage, u, part, me, me)
+        pltpu.make_async_copy(source, target, own_sem.at[u, part]).start()
+
         def send(step, carry):
             to = lax.rem(me + step, devices)
-            source, target = parts(u, ch, to, me)
+            source, target = ends(stage, u, part, to, me)
             pltpu.make_async_remote_copy(
                 src_ref=source,
                 dst_ref=target,
-                send_sem=ssem.at[u, ch],
-                recv_sem=rsem.at[u, ch],
-                device_id=place(to),
-                device_id_type=MESH,
+                send_sem=ssem.at[u, part],
+                recv_sem=rsem.at[u, part],
+                device_id=to,
+                device_id_type=LOGICAL,
             ).start()
             return carry
 
-        lax.fori_loop(1, devices, send, 0)
-        source, target = parts(u, ch, me, me)
-        own = pltpu.make_async_copy(source, target, own_sem)
-        own.start()
-        own.wait()
-
-    def arrival(parts, u, ch, ssem, rsem):
-        source, target = parts(u, ch, pl.ds(0, devices - 1), pl.ds(0, devices - 1))
+        lax.fori_loop(1, devices, send, 0, unroll=UNROLL)
+
+    def all_of(stage, u, part):
+        ssem, rsem = stage[3:5]
+        others = pl.ds(0, devices - 1)
+        source, target = ends(stage, u, part, others, others)
         return pltpu.make_async_remote_copy(
             src_ref=source,
             dst_ref=target,
-            send_sem=ssem.at[u, ch],
-            recv_sem=rsem.at[u, ch],
-            device_id=place(me),
-            device_id_type=MESH,
+            send_sem=ssem.at[u, part],
+            recv_sem=rsem.at[u, part],
+            device_id=me,
+            device_id_type=LOGICAL,
         )
 
+    def receive(stage, u, part):
+        source, target = ends(stage, u, part, me, me)
+        pltpu.make_async_copy(source, target, stage[5].at[u, part]).wait()
+        all_of(stage, u, part).wait_recv()
+
     def plane_of(u, cb, side):
-        return edge_recv.at[u, cb, side].reshape(plane, LANES)
+        return edge_recv.at[u, 2 * cb + side].reshape(plane, LANES)
 
     fetched("embed", "in_gain", "in_bias", "left", "right", "gate")
     for k in range(2):
         cols[8 + k] = column(embed_ref[k : k + 1, :])
     prepare_in(0)
     fetched("x", "chain", "own_chain", "mask")
-    for ch in range(CHUNKS):
-        for cb in range(ch * per, (ch + 1) * per):
+    for part, (low, high) in enumerate(EDGE_PARTS[0]):
+        for cb in range(low // 2, high // 2):
             load(cb)
             edges(0, cb)
-        if ch == 0:
+        if part == 0:
             pl.semaphore_wait(barrier, devices - 1)
-        send_all(edge_parts, 0, ch, edge_ssem, edge_rsem)
+        send_all(edge_stage, 0, part)
+    for cb in range(blocks):
+        gate(0, cb)
     fetched("out_gain", "out_bias", "out_w")
     prepare_out(0)
     prepare_in(1)
     prepare_out(1)
 
+    for part in range(len(EDGE_PARTS[0])):
+        receive(edge_stage, 0, part)
+    left = jnp.concatenate([plane_of(0, cb, 0)[...] for cb in range(blocks)], axis=1)
+    for part, (low, high) in enumerate(PROD_PARTS[0]):
+        for jb in range(low, high):
+            span = slice(jb * LANES, (jb + 1) * LANES)
+            right = jnp.concatenate(
+                [plane_of(0, cb, 1)[span, :] for cb in range(blocks)], axis=1
+            )
+            prod_send.at[0, jb].reshape(plane, LANES)[...] = dot(left, right, NT).astype(BF16)
+        send_all(prod_stage, 0, part)
+
+    sent = 0
+    for part, (low, high) in enumerate(PROD_PARTS[0]):
+        receive(prod_stage, 0, part)
+        for cb in range(low, high):
+            finish(0, cb)
+            edges(1, cb)
+        while sent < len(EDGE_PARTS[1]) and EDGE_PARTS[1][sent][1] <= 2 * high:
+            send_all(edge_stage, 1, sent)
+            sent += 1
+        for cb in range(low, high):
+            gate(1, cb)
+
+    done = 0
+    for part, (low, high) in enumerate(EDGE_PARTS[1]):
+        receive(edge_stage, 1, part)
+        for item in range(low, high):
+            if item % 2 == 0:
+                cb = item // 2
+                left_t[cb * LANES : (cb + 1) * LANES, :] = jnp.transpose(plane_of(1, cb, 0)[...])
+        if high < 2 * blocks - 1:
+            continue
+        while done < len(PROD_PARTS[1]) and 2 * PROD_PARTS[1][done][1] <= high:
+            for jb in range(*PROD_PARTS[1][done]):
+                product = dot(left_t[...], plane_of(1, jb, 1)[...], NN)
+                prod_send.at[1, jb].reshape(plane, LANES)[...] = product.astype(BF16)
+            send_all(prod_stage, 1, done)
+            done += 1
+
+    for part, (low, high) in enumerate(PROD_PARTS[1]):
+        receive(prod_stage, 1, part)
+        for cb in range(low, high):
+            finish(1, cb)
     for u in range(2):
-        if u == 0:
-            for ch in range(CHUNKS):
-                arrival(edge_parts, u, ch, edge_ssem, edge_rsem).wait_recv()
-            left = jnp.concatenate([plane_of(0, cb, 0)[...] for cb in range(blocks)], axis=1)
-        else:
-            for ch in range(CHUNKS):
-                arrival(edge_parts, u, ch, edge_ssem, edge_rsem).wait_recv()
-                for cb in range(ch * per, (ch + 1) * per):
-                    left_t[cb * LANES : (cb + 1) * LANES, :] = jnp.transpose(plane_of(1, cb, 0)[...])
-            left = left_t[...]
-        for ch in range(CHUNKS):
-            for jb in range(ch * per, (ch + 1) * per):
-                if u == 0:
-                    right = jnp.concatenate(
-                        [
-                            plane_of(0, cb, 1)[jb * LANES : (jb + 1) * LANES, :]
-                            for cb in range(blocks)
-                        ],
-                        axis=1,
-                    )
-                    product = dot(left, right, NT)
-                else:
-                    product = dot(left, plane_of(1, jb, 1)[...], NN)
-                prod_send.at[u, jb].reshape(plane, LANES)[...] = product.astype(BF16)
-            send_all(prod_parts, u, ch, prod_ssem, prod_rsem)
-        for ch in range(CHUNKS):
-            arrival(prod_parts, u, ch, prod_ssem, prod_rsem).wait_recv()
-            for cb in range(ch * per, (ch + 1) * per):
-                finish(u, cb)
-                if u == 0:
-                    edges(1, cb)
-            if u == 0:
-                send_all(edge_parts, 1, ch, edge_ssem, edge_rsem)
-    for u in range(2):
-        for ch in range(CHUNKS):
-            arrival(edge_parts, u, ch, edge_ssem, edge_rsem).wait_send()
-            arrival(prod_parts, u, ch, prod_ssem, prod_rsem).wait_send()
+        for stage in (edge_stage, prod_stage):
+            for part in range(len(stage[0][u])):
+                all_of(stage, u, part).wait_send()
 
 
 def shards(
@@ -327,18 +351,20 @@
             pltpu.VMEM((2, LANES, LANES), BF16),
             pltpu.VMEM((blocks, chan, wide), F32),
             pltpu.VMEM((blocks, chan, wide), F32),
+            pltpu.VMEM((blocks, chan, wide), BF16),
             pltpu.VMEM((blocks, 1, wide), F32),
             pltpu.VMEM((2, LANES * rows, LANES), F32),
             pltpu.VMEM((columns, devices * rows), BF16),
-            pltpu.VMEM((2, blocks, 2, LANES, rows, LANES), BF16),
-            pltpu.VMEM((2, blocks, 2, devices, rows, LANES), BF16),
+            pltpu.VMEM((2, 2 * blocks, LANES, rows, LANES), BF16),
+            pltpu.VMEM((2, 2 * blocks, devices, rows, LANES), BF16),
             pltpu.VMEM((2, blocks, devices, rows, LANES), BF16),
             pltpu.VMEM((2, blocks, LANES, rows, LANES), BF16),
-            pltpu.SemaphoreType.DMA((2, CHUNKS)),
-            pltpu.SemaphoreType.DMA((2, CHUNKS)),
-            pltpu.SemaphoreType.DMA((2, CHUNKS)),
-            pltpu.SemaphoreType.DMA((2, CHUNKS)),
-            pltpu.SemaphoreType.DMA,
+            pltpu.SemaphoreType.DMA((2, MOST)),
+            pltpu.SemaphoreType.DMA((2, MOST)),
+            pltpu.SemaphoreType.DMA((2, MOST)),
+            pltpu.SemaphoreType.DMA((2, MOST)),
+            pltpu.SemaphoreType.DMA((2, MOST)),
+            pltpu.SemaphoreType.DMA((2, MOST)),
         ],
         compiler_params=pltpu.CompilerParams(
             collective_id=0, has_side_effects=True, vmem_limit_bytes=40 * 1024 * 1024

time: 66.4 us -> 62.6 us (0.943)
  Pallas kernels: 65.5 us -> 61.7 us
    pallas_call x1, Pallas kernels: 65.5 us -> 61.7 us  [shards(): pl.pallas_call(body, out_shape=jax.ShapeDtypeStruct((rows, columns, chan)...]
where the time goes in v3:
time: 62.6 us; the launch traced here: 62.5 us
  Pallas kernels  61.7 us (99%)
  local copies, waits for them, and re-layouts  0.8 us (1%)
    pallas_call x1, Pallas kernels, shards(): pl.pallas_call(body, out_shape=jax.ShapeDtypeStruct((rows, columns, chan)...  61.7 us

profile of v3, /device:TPU:1, one launch (start us, length us, event | category | flops | bytes accessed | tf_op | source)
XLA Modules:
  0.0 62.5 jit_solution(14267495004701509309)
XLA Ops:
  0.0 61.7 %triangle_updates.1 = bf16[4,512,128]{2,1,0:T(8,128)(2,1)S(1)} custom-call(bf16[4,512,128]{2,1,0:T(8,128)(2,1)} %x_hbm.1, s32[4,512]{1,0:T(4,128)} %mask_hbm.1, s32[512]{0:T(512)} %chain_hbm.1, f32[2,128]{1,0:T(2,128)} %embed_hbm.1, f32[2,128]{1,0:T(2,128)} %in_gain_hbm.1, f32[2,128]{1,0:T(2,128)} %in_bias_hbm.1, bf16[2,128,256]{2,1,0:T(8,128)(2,1)} %left_hbm.1, ...), custom_call_target="tpu_custom_call" | custom-call | tf_op jit(solution)/shard_map/triangle_updates/pallas_call | solution.py:340
  61.7 0.8 %copy.14 = bf16[4,512,128]{2,1,0:T(8,128)(2,1)} copy(bf16[4,512,128]{2,1,0:T(8,128)(2,1)S(1)} %triangle_updates.1) | data formatting | bytes 1048576

commit v4 on v3

v4 whole, which is shorter than its diff:
```python
import jax
import jax.numpy as jnp
from jax import lax
from jax.experimental import pallas as pl
from jax.experimental.pallas import tpu as pltpu
from jax.sharding import PartitionSpec as P

F32, BF16 = jnp.float32, jnp.bfloat16
LOGICAL = pl.DeviceIdType.LOGICAL
LANES = 128
UNROLL = 8
NN, NT = ((1,), (0,)), ((1,), (1,))
LEFT, RIGHT = 0, 1
MOVES = (
    ("right0", 0, 2),
    ("right0", 2, 2),
    ("left0", 0, 4),
    ("left0", 4, 4),
    ("prod0", 0, 4),
    ("prod0", 4, 4),
    ("edge1", 0, 6),
    ("edge1", 6, 6),
    ("edge1", 12, 4),
    ("prod1", 0, 1),
    ("prod1", 1, 1),
    ("prod1", 2, 2),
)
SLOT = (((0, 1, 2, 3), (6, 7, 8, 9)), ((4, 5, 12, 13), (10, 11, 14, 15)))


def dot(a, b, dims):
    return lax.dot_general(a, b, (dims, ((), ())), preferred_element_type=F32)


def layer_norm(values, gain, bias):
    average = jnp.mean(values, axis=0, keepdims=True)
    centered = values - average
    variance = jnp.mean(centered * centered, axis=0, keepdims=True)
    return (centered * lax.rsqrt(variance + 1e-05) * gain + bias).astype(BF16)


def body(
    x_hbm,
    mask_hbm,
    chain_hbm,
    embed_hbm,
    in_gain_hbm,
    in_bias_hbm,
    left_hbm,
    right_hbm,
    gate_hbm,
    out_gain_hbm,
    out_bias_hbm,
    out_w_hbm,
    out_ref,
    x_ref,
    mask_ref,
    chain_ref,
    embed_ref,
    in_gain_ref,
    in_bias_ref,
    left_ref,
    right_ref,
    gate_ref,
    out_gain_ref,
    out_bias_ref,
    out_w_ref,
    own_chain_ref,
    in_sems,
    cols,
    w_in,
    w_out,
    state,
    gating,
    normed_rows,
    spread,
    left_t,
    right0_send,
    right0_recv,
    left0_send,
    left0_recv,
    prod0_send,
    prod0_recv,
    edge1_send,
    edge1_recv,
    prod1_send,
    prod1_recv,
    send_sems,
    recv_sems,
    own_sems,
):
    rows, columns, chan = x_hbm.shape
    blocks = columns // LANES
    pairs = rows // 2
    blk_count = lax.axis_size("blk")
    devices = lax.axis_size("grp") * blk_count
    plane = devices * rows
    half = devices * 2
    me = lax.axis_index("grp") * blk_count + lax.axis_index("blk")
    buffers = {
        "right0": (right0_send, right0_recv),
        "left0": (left0_send, left0_recv),
        "prod0": (prod0_send, prod0_recv),
        "edge1": (edge1_send, edge1_recv),
        "prod1": (prod1_send, prod1_recv),
    }

    loads = {}

    def fetch(name, source, target):
        loads[name] = pltpu.make_async_copy(source, target, in_sems.at[len(loads)])
        loads[name].start()

    def fetched(*wanted):
        for name in wanted:
            loads[name].wait()

    fetch("embed", embed_hbm, embed_ref)
    fetch("in_gain", in_gain_hbm, in_gain_ref)
    fetch("in_bias", in_bias_hbm, in_bias_ref)
    fetch("left", left_hbm, left_ref)
    fetch("right", right_hbm, right_ref)
    fetch("gate", gate_hbm, gate_ref)
    fetch("x", x_hbm, x_ref)
    fetch("chain", chain_hbm, chain_ref)
    fetch("own_chain", chain_hbm, own_chain_ref)
    fetch("mask", mask_hbm, mask_ref)
    fetch("out_gain", out_gain_hbm, out_gain_ref)
    fetch("out_bias", out_bias_hbm, out_bias_ref)
    fetch("out_w", out_w_hbm, out_w_ref)

    barrier = pltpu.get_barrier_semaphore()

    def greet(step, carry):
        pl.semaphore_signal(
            barrier, inc=1, device_id=lax.rem(me + step, devices), device_id_type=LOGICAL
        )
        return carry

    lax.fori_loop(1, devices, greet, 0, unroll=UNROLL)

    eye = (
        lax.broadcasted_iota(jnp.int32, (LANES, LANES), 0)
        == lax.broadcasted_iota(jnp.int32, (LANES, LANES), 1)
    ).astype(BF16)

    def column(vector):
        return jnp.transpose(jnp.broadcast_to(vector, (LANES, chan)))

    def four(block):
        return jnp.concatenate([block] * 4, axis=1)

    def lanes(index):
        return slice(index * LANES, (index + 1) * LANES)

    def prepare_out(u):
        cols[4 * u + 2] = column(out_gain_ref[u : u + 1, :])
        cols[4 * u + 3] = column(out_bias_ref[u : u + 1, :])
        w_out[u] = jnp.transpose(out_w_ref[u])

    def prepare_in(u):
        cols[4 * u] = column(in_gain_ref[u : u + 1, :])
        cols[4 * u + 1] = column(in_bias_ref[u : u + 1, :])
        for k in range(2):
            w_in[u, lanes(k), :] = jnp.transpose(left_ref[u, :, lanes(k)])
            w_in[u, lanes(2 + k), :] = jnp.transpose(right_ref[u, :, lanes(k)])
        w_in[u, lanes(4), :] = jnp.transpose(gate_ref[u])

    def load(cb):
        other, same = cols[8], cols[9]
        for r in range(rows):
            flat = dot(eye, x_ref[r, lanes(cb), :], NT)
            together = chain_ref[pl.ds(cb * LANES, LANES)][None, :] == own_chain_ref[me * rows + r]
            state[r, :, lanes(cb)] = flat + jnp.where(together, same, other)

    def edge(u, side, normed, mask):
        low = 2 * side
        gate = dot(w_in[u, lanes(low), :], normed, NN)
        value = dot(w_in[u, lanes(low + 1), :], normed, NN)
        return jax.nn.sigmoid(gate) * value * mask

    def edges_of_columns(cb):
        values = jnp.concatenate([state[r, :, lanes(cb)] for r in range(rows)], axis=1)
        mask = jnp.concatenate([mask_ref[r : r + 1, lanes(cb)] for r in range(rows)], axis=1)
        mask = mask.astype(F32)
        normed = layer_norm(values, four(cols[0]), four(cols[1]))
        for r in range(rows):
            normed_rows[r, :, lanes(cb)] = normed[:, lanes(r)]
        value = edge(0, RIGHT, normed, mask)
        for r in range(rows):
            spread[0, pl.ds(r, LANES, stride=rows), :] = value[:, lanes(r)]
        right0_send.at[cb].reshape(LANES * rows, LANES)[...] = spread[
            0, : LANES * rows, :
        ].astype(BF16)
        value = edge(0, LEFT, normed, mask)
        for pair in range(pairs):
            low = pair * 2 * LANES
            for r in range(2):
                spread[1, pl.ds(low + r, LANES, stride=2), :] = value[:, lanes(2 * pair + r)]
            left0_send.at[pair * blocks + cb].reshape(LANES * 2, LANES)[...] = spread[
                1, low : low + 2 * LANES, :
            ].astype(BF16)

    def edges_of_pair(pair):
        for r in range(2):
            row = 2 * pair + r
            mask = mask_ref[row : row + 1, :].astype(F32)
            normed = layer_norm(state[row], four(cols[4]), four(cols[5]))
            normed_rows[row] = normed
            for side in (LEFT, RIGHT):
                value = edge(1, side, normed, mask)
                for cb in range(blocks):
                    low = cb * 2 * LANES
                    spread[2 + side, pl.ds(low + r, LANES, stride=2), :] = value[:, lanes(cb)]
        for side in (LEFT, RIGHT):
            for cb in range(blocks):
                low = cb * 2 * LANES
                edge1_send.at[SLOT[side][pair][cb]].reshape(LANES * 2, LANES)[...] = spread[
                    2 + side, low : low + 2 * LANES, :
                ].astype(BF16)

    def gates(u, row):
        gating[row] = jax.nn.sigmoid(dot(w_in[u, lanes(4), :], normed_rows[row], NN))

    def updated(u, product, values, gate):
        normed = layer_norm(product, four(cols[4 * u + 2]), four(cols[4 * u + 3]))
        return (values + gate * dot(w_out[u], normed, NN)).astype(BF16)

    def finish_pair(pair):
        for jb in range(blocks):
            low = jb * 2 * LANES
            spread[0, low : low + 2 * LANES, :] = (
                prod0_recv.at[pair * blocks + jb].reshape(LANES * 2, LANES)[...].astype(F32)
            )
        for r in range(2):
            row = 2 * pair + r
            product = jnp.concatenate(
                [
                    spread[0, pl.ds(jb * 2 * LANES + r, LANES, stride=2), :]
                    for jb in range(blocks)
                ],
                axis=1,
            )
            state[row] = updated(0, product, state[row], gating[row]).astype(F32)

    def finish_columns(cb):
        spread[0, : LANES * rows, :] = (
            prod1_recv.at[cb].reshape(LANES * rows, LANES)[...].astype(F32)
        )
        product = jnp.concatenate(
            [spread[0, pl.ds(r, LANES, stride=rows), :] for r in range(rows)], axis=1
        )
        values = jnp.concatenate([state[r, :, lanes(cb)] for r in range(rows)], axis=1)
        gate = jnp.concatenate([gating[r, :, lanes(cb)] for r in range(rows)], axis=1)
        new = updated(1, product, values, gate)
        for r in range(rows):
            out_ref[r, lanes(cb), :] = dot(eye, new[:, lanes(r)], NT).astype(BF16)

    def ends(move, source, target):
        name, low, count = MOVES[move]
        sent, received = buffers[name]
        span = pl.ds(low, count)
        return sent.at[span, source], received.at[span, target]

    def send_all(move):
        source, target = ends(move, me, me)
        pltpu.make_async_copy(source, target, own_sems.at[move]).start()

        def send(step, carry):
            to = lax.rem(me + step, devices)
            source, target = ends(move, to, me)
            pltpu.make_async_remote_copy(
                src_ref=source,
                dst_ref=target,
                send_sem=send_sems.at[move],
                recv_sem=recv_sems.at[move],
                device_id=to,
                device_id_type=LOGICAL,
            ).start()
            return carry

        lax.fori_loop(1, devices, send, 0, unroll=UNROLL)

    def all_of(move):
        others = pl.ds(0, devices - 1)
        source, target = ends(move, others, others)
        return pltpu.make_async_remote_copy(
            src_ref=source,
            dst_ref=target,
            send_sem=send_sems.at[move],
            recv_sem=recv_sems.at[move],
            device_id=me,
            device_id_type=LOGICAL,
        )

    def receive(move):
        source, target = ends(move, me, me)
        pltpu.make_async_copy(source, target, own_sems.at[move]).wait()
        all_of(move).wait_recv()

    fetched("embed", "in_gain", "in_bias", "left", "right", "gate")
    for k in range(2):
        cols[8 + k] = column(embed_ref[k : k + 1, :])
    prepare_in(0)
    fetched("x", "chain", "own_chain", "mask")
    for cb in range(blocks):
        load(cb)
        edges_of_columns(cb)
        if cb == 1:
            pl.semaphore_wait(barrier, devices - 1)
            send_all(0)
    send_all(1)
    send_all(2)
    send_all(3)
    for row in range(rows):
        gates(0, row)
    fetched("out_gain", "out_bias", "out_w")
    prepare_out(0)
    prepare_in(1)
    prepare_out(1)

    receive(0)
    receive(1)
    for pair in range(pairs):
        receive(2 + pair)
        left = jnp.concatenate(
            [left0_recv.at[pair * blocks + cb].reshape(half, LANES)[...] for cb in range(blocks)],
            axis=1,
        )
        for jb in range(blocks):
            right = jnp.concatenate(
                [
                    right0_recv.at[cb].reshape(plane, LANES)[lanes(jb), :]
                    for cb in range(blocks)
                ],
                axis=1,
            )
            prod0_send.at[pair * blocks + jb].reshape(half, LANES)[...] = dot(
                left, right, NT
            ).astype(BF16)
        send_all(4 + pair)

    for pair in range(pairs):
        receive(4 + pair)
        finish_pair(pair)
        edges_of_pair(pair)
        send_all(6 + pair)
        if pair == pairs - 1:
            send_all(8)
        for r in range(2):
            gates(1, 2 * pair + r)

    for pair in range(pairs):
        receive(6 + pair)
        span = slice(pair * half, (pair + 1) * half)
        for cb in range(blocks):
            left_t[lanes(cb), span] = jnp.transpose(
                edge1_recv.at[SLOT[LEFT][pair][cb]].reshape(half, LANES)[...]
            )
    for move in (9, 10, 11):
        if move == 11:
            receive(8)
        for jb in range(MOVES[move][1], MOVES[move][1] + MOVES[move][2]):
            right = jnp.concatenate(
                [
                    edge1_recv.at[SLOT[RIGHT][pair][jb]].reshape(half, LANES)[...]
                    for pair in range(pairs)
                ],
                axis=0,
            )
            prod1_send.at[jb].reshape(plane, LANES)[...] = dot(left_t[...], right, NN).astype(BF16)
        send_all(move)
    for move in (9, 10, 11):
        receive(move)
        for cb in range(MOVES[move][1], MOVES[move][1] + MOVES[move][2]):
            finish_columns(cb)
    for move in range(len(MOVES)):
        all_of(move).wait_send()


def shards(
    pair_repr,
    pair_mask,
    chain_index,
    entity_embed,
    input_gain,
    input_bias,
    left_weight,
    right_weight,
    gate_weight,
    output_gain,
    output_bias,
    output_weight,
):
    rows, columns, chan = pair_repr.shape
    devices = lax.axis_size("grp") * lax.axis_size("blk")
    blocks = columns // LANES
    pairs = rows // 2
    count = len(MOVES)
    arguments = (
        pair_repr,
        pair_mask,
        chain_index,
        entity_embed,
        input_gain,
        input_bias,
        left_weight,
        right_weight,
        gate_weight,
        output_gain,
        output_bias,
        output_weight,
    )
    return pl.pallas_call(
        body,
        out_shape=jax.ShapeDtypeStruct((rows, columns, chan), BF16),
        in_specs=[pl.BlockSpec(memory_space=pltpu.HBM)] * len(arguments),
        out_specs=pl.BlockSpec(memory_space=pltpu.VMEM),
        scratch_shapes=[pltpu.VMEM(a.shape, a.dtype) for a in arguments]
        + [
            pltpu.SMEM(chain_index.shape, chain_index.dtype),
            pltpu.SemaphoreType.DMA((len(arguments) + 1,)),
            pltpu.VMEM((10, LANES, LANES), F32),
            pltpu.VMEM((2, 5 * LANES, chan), BF16),
            pltpu.VMEM((2, LANES, LANES), BF16),
            pltpu.VMEM((rows, chan, columns), F32),
            pltpu.VMEM((rows, chan, columns), F32),
            pltpu.VMEM((rows, chan, columns), BF16),
            pltpu.VMEM((4, 2 * LANES * blocks, LANES), F32),
            pltpu.VMEM((columns, devices * rows), BF16),
            pltpu.VMEM((blocks, LANES, rows, LANES), BF16),
            pltpu.VMEM((blocks, devices, rows, LANES), BF16),
            pltpu.VMEM((pairs * blocks, LANES, 2, LANES), BF16),
            pltpu.VMEM((pairs * blocks, devices, 2, LANES), BF16),
            pltpu.VMEM((pairs * blocks, devices, 2, LANES), BF16),
            pltpu.VMEM((pairs * blocks, LANES, 2, LANES), BF16),
            pltpu.VMEM((2 * pairs * blocks, LANES, 2, LANES), BF16),
            pltpu.VMEM((2 * pairs * blocks, devices, 2, LANES), BF16),
            pltpu.VMEM((blocks, devices, rows, LANES), BF16),
            pltpu.VMEM((blocks, LANES, rows, LANES), BF16),
            pltpu.SemaphoreType.DMA((count,)),
            pltpu.SemaphoreType.DMA((count,)),
            pltpu.SemaphoreType.DMA((count,)),
        ],
        compiler_params=pltpu.CompilerParams(
            collective_id=0, has_side_effects=True, vmem_limit_bytes=40 * 1024 * 1024
        ),
        name="triangle_updates",
    )(*[pltpu.with_memory_space_constraint(a, pltpu.HBM) for a in arguments])


def solution(mesh):
    rows = P(("grp", "blk"), None, None)
    placed = (rows, P(("grp", "blk"), None)) + (P(),) * 10
    return jax.shard_map(shards, mesh=mesh, in_specs=placed, out_specs=rows, check_vma=False)
```

time: 62.6 us -> 60.5 us (0.966)
  Pallas kernels: 61.7 us -> 59.6 us
    pallas_call x1, Pallas kernels: 61.7 us -> 59.6 us  [shards(): pl.pallas_call(body, out_shape=jax.ShapeDtypeStruct((rows, columns, chan)...]
where the time goes in v4:
time: 60.5 us; the launch traced here: 60.4 us
  Pallas kernels  59.6 us (99%)
  local copies, waits for them, and re-layouts  0.8 us (1%)
    pallas_call x1, Pallas kernels, shards(): pl.pallas_call(body, out_shape=jax.ShapeDtypeStruct((rows, columns, chan)...  59.6 us

profile of v4, /device:TPU:1, one launch (start us, length us, event | category | flops | bytes accessed | tf_op | source)
XLA Modules:
  0.0 60.4 jit_solution(1040565193363521600)
XLA Ops:
  0.0 59.6 %triangle_updates.1 = bf16[4,512,128]{2,1,0:T(8,128)(2,1)S(1)} custom-call(bf16[4,512,128]{2,1,0:T(8,128)(2,1)} %x_hbm.1, s32[4,512]{1,0:T(4,128)} %mask_hbm.1, s32[512]{0:T(512)} %chain_hbm.1, f32[2,128]{1,0:T(2,128)} %embed_hbm.1, f32[2,128]{1,0:T(2,128)} %in_gain_hbm.1, f32[2,128]{1,0:T(2,128)} %in_bias_hbm.1, bf16[2,128,256]{2,1,0:T(8,128)(2,1)} %left_hbm.1, ...), custom_call_target="tpu_custom_call" | custom-call | tf_op jit(solution)/shard_map/triangle_updates/pallas_call | solution.py:414
  59.6 0.8 %copy.14 = bf16[4,512,128]{2,1,0:T(8,128)(2,1)} copy(bf16[4,512,128]{2,1,0:T(8,128)(2,1)S(1)} %triangle_updates.1) | data formatting | bytes 1048576

commit v5 on v4

--- a/solution.py
+++ b/solution.py
@@ -16,16 +16,17 @@
     ("right0", 2, 2),
     ("left0", 0, 4),
     ("left0", 4, 4),
-    ("prod0", 0, 4),
+    ("prod0", 0, 2),
+    ("prod0", 2, 2),
     ("prod0", 4, 4),
-    ("edge1", 0, 6),
+    ("edge1", 0, 4),
+    ("edge1", 4, 2),
     ("edge1", 6, 6),
     ("edge1", 12, 4),
-    ("prod1", 0, 1),
-    ("prod1", 1, 1),
+    ("prod1", 0, 2),
     ("prod1", 2, 2),
 )
-SLOT = (((0, 1, 2, 3), (6, 7, 8, 9)), ((4, 5, 12, 13), (10, 11, 14, 15)))
+SLOT = (((0, 1, 4, 5), (6, 7, 8, 9)), ((2, 3, 12, 14), (10, 11, 13, 15)))
 
 
 def dot(a, b, dims):
@@ -147,8 +148,8 @@
     def column(vector):
         return jnp.transpose(jnp.broadcast_to(vector, (LANES, chan)))
 
-    def four(block):
-        return jnp.concatenate([block] * 4, axis=1)
+    def wide(block, count):
+        return jnp.concatenate([block] * count, axis=1)
 
     def lanes(index):
         return slice(index * LANES, (index + 1) * LANES)
@@ -183,7 +184,7 @@
         values = jnp.concatenate([state[r, :, lanes(cb)] for r in range(rows)], axis=1)
         mask = jnp.concatenate([mask_ref[r : r + 1, lanes(cb)] for r in range(rows)], axis=1)
         mask = mask.astype(F32)
-        normed = layer_norm(values, four(cols[0]), four(cols[1]))
+        normed = layer_norm(values, wide(cols[0], rows), wide(cols[1], rows))
         for r in range(rows):
             normed_rows[r, :, lanes(cb)] = normed[:, lanes(r)]
         value = edge(0, RIGHT, normed, mask)
@@ -201,19 +202,22 @@
                 1, low : low + 2 * LANES, :
             ].astype(BF16)
 
-    def edges_of_pair(pair):
+    def edges_of_pair(pair, spots):
+        span = slice(spots[0] * LANES, (spots[-1] + 1) * LANES)
         for r in range(2):
             row = 2 * pair + r
-            mask = mask_ref[row : row + 1, :].astype(F32)
-            normed = layer_norm(state[row], four(cols[4]), four(cols[5]))
-            normed_rows[row] = normed
+            mask = mask_ref[row : row + 1, span].astype(F32)
+            normed = layer_norm(
+                state[row, :, span], wide(cols[4], len(spots)), wide(cols[5], len(spots))
+            )
+            normed_rows[row, :, span] = normed
             for side in (LEFT, RIGHT):
                 value = edge(1, side, normed, mask)
-                for cb in range(blocks):
+                for k, cb in enumerate(spots):
                     low = cb * 2 * LANES
-                    spread[2 + side, pl.ds(low + r, LANES, stride=2), :] = value[:, lanes(cb)]
+                    spread[2 + side, pl.ds(low + r, LANES, stride=2), :] = value[:, lanes(k)]
         for side in (LEFT, RIGHT):
-            for cb in range(blocks):
+            for cb in spots:
                 low = cb * 2 * LANES
                 edge1_send.at[SLOT[side][pair][cb]].reshape(LANES * 2, LANES)[...] = spread[
                     2 + side, low : low + 2 * LANES, :
@@ -223,11 +227,14 @@
         gating[row] = jax.nn.sigmoid(dot(w_in[u, lanes(4), :], normed_rows[row], NN))
 
     def updated(u, product, values, gate):
-        normed = layer_norm(product, four(cols[4 * u + 2]), four(cols[4 * u + 3]))
+        count = product.shape[1] // LANES
+        gain, bias = wide(cols[4 * u + 2], count), wide(cols[4 * u + 3], count)
+        normed = layer_norm(product, gain, bias)
         return (values + gate * dot(w_out[u], normed, NN)).astype(BF16)
 
-    def finish_pair(pair):
-        for jb in range(blocks):
+    def finish_pair(pair, spots):
+        span = slice(spots[0] * LANES, (spots[-1] + 1) * LANES)
+        for jb in spots:
             low = jb * 2 * LANES
             spread[0, low : low + 2 * LANES, :] = (
                 prod0_recv.at[pair * blocks + jb].reshape(LANES * 2, LANES)[...].astype(F32)
@@ -235,13 +242,12 @@
         for r in range(2):
             row = 2 * pair + r
             product = jnp.concatenate(
-                [
-                    spread[0, pl.ds(jb * 2 * LANES + r, LANES, stride=2), :]
-                    for jb in range(blocks)
-                ],
+                [spread[0, pl.ds(jb * 2 * LANES + r, LANES, stride=2), :] for jb in spots],
                 axis=1,
             )
-            state[row] = updated(0, product, state[row], gating[row]).astype(F32)
+            state[row, :, span] = updated(
+                0, product, state[row, :, span], gating[row, :, span]
+            ).astype(F32)
 
     def finish_columns(cb):
         spread[0, : LANES * rows, :] = (
@@ -319,15 +325,9 @@
     prepare_in(1)
     prepare_out(1)
 
-    receive(0)
-    receive(1)
-    for pair in range(pairs):
-        receive(2 + pair)
-        left = jnp.concatenate(
-            [left0_recv.at[pair * blocks + cb].reshape(half, LANES)[...] for cb in range(blocks)],
-            axis=1,
-        )
-        for jb in range(blocks):
+    def products_of_pair(pair, move):
+        for slot in spots_of(move):
+            jb = slot - pair * blocks
             right = jnp.concatenate(
                 [
                     right0_recv.at[cb].reshape(plane, LANES)[lanes(jb), :]
@@ -335,32 +335,53 @@
                 ],
                 axis=1,
             )
-            prod0_send.at[pair * blocks + jb].reshape(half, LANES)[...] = dot(
-                left, right, NT
-            ).astype(BF16)
-        send_all(4 + pair)
-
-    for pair in range(pairs):
-        receive(4 + pair)
-        finish_pair(pair)
-        edges_of_pair(pair)
-        send_all(6 + pair)
-        if pair == pairs - 1:
-            send_all(8)
-        for r in range(2):
-            gates(1, 2 * pair + r)
-
-    for pair in range(pairs):
-        receive(6 + pair)
-        span = slice(pair * half, (pair + 1) * half)
-        for cb in range(blocks):
-            left_t[lanes(cb), span] = jnp.transpose(
-                edge1_recv.at[SLOT[LEFT][pair][cb]].reshape(half, LANES)[...]
-            )
-    for move in (9, 10, 11):
-        if move == 11:
-            receive(8)
-        for jb in range(MOVES[move][1], MOVES[move][1] + MOVES[move][2]):
+            left = jnp.concatenate(
+                [
+                    left0_recv.at[pair * blocks + cb].reshape(half, LANES)[...]
+                    for cb in range(blocks)
+                ],
+                axis=1,
+            )
+            prod0_send.at[slot].reshape(half, LANES)[...] = dot(left, right, NT).astype(BF16)
+        send_all(move)
+
+    def spots_of(move):
+        name, low, count = MOVES[move]
+        return tuple(range(low, low + count))
+
+    receive(0)
+    receive(1)
+    receive(2)
+    products_of_pair(0, 4)
+    products_of_pair(0, 5)
+    receive(3)
+    products_of_pair(1, 6)
+
+    for move, pair, then in ((4, 0, (7,)), (5, 0, (8,)), (6, 1, (9, 10))):
+        spots = tuple(slot - pair * blocks for slot in spots_of(move))
+        receive(move)
+        finish_pair(pair, spots)
+        edges_of_pair(pair, spots)
+        for following in then:
+            send_all(following)
+    for row in range(rows):
+        gates(1, row)
+
+    for move in (7, 8, 9):
+        receive(move)
+        for pair in range(pairs):
+            for cb in range(blocks):
+                if SLOT[LEFT][pair][cb] in spots_of(move):
+                    left_t[lanes(cb), pair * half : (pair + 1) * half] = jnp.transpose(
+                        edge1_recv.at[SLOT[LEFT][pair][cb]].reshape(half, LANES)[...]
+                    )
+    arrived = 12
+    for move in range(11, len(MOVES)):
+        for jb in spots_of(move):
+            for last in (10,):
+                if SLOT[RIGHT][0][jb] in spots_of(last) and arrived <= SLOT[RIGHT][1][jb]:
+                    receive(last)
+                    arrived = spots_of(last)[-1] + 1
             right = jnp.concatenate(
                 [
                     edge1_recv.at[SLOT[RIGHT][pair][jb]].reshape(half, LANES)[...]
@@ -370,9 +391,9 @@
             )
             prod1_send.at[jb].reshape(plane, LANES)[...] = dot(left_t[...], right, NN).astype(BF16)
         send_all(move)
-    for move in (9, 10, 11):
+    for move in range(11, len(MOVES)):
         receive(move)
-        for cb in range(MOVES[move][1], MOVES[move][1] + MOVES[move][2]):
+        for cb in spots_of(move):
             finish_columns(cb)
     for move in range(len(MOVES)):
         all_of(move).wait_send()

time: 60.5 us -> 58.9 us (0.974)
  Pallas kernels: 59.6 us -> 58 us
    pallas_call x1, Pallas kernels: 59.6 us -> 58 us  [shards(): pl.pallas_call(body, out_shape=jax.ShapeDtypeStruct((rows, columns, chan)...]
where the time goes in v5:
time: 58.9 us; the launch traced here: 58.8 us
  Pallas kernels  58 us (98%)
  local copies, waits for them, and re-layouts  0.8 us (1%)
    pallas_call x1, Pallas kernels, shards(): pl.pallas_call(body, out_shape=jax.ShapeDtypeStruct((rows, columns, chan)...  58 us

profile of v5, /device:TPU:1, one launch (start us, length us, event | category | flops | bytes accessed | tf_op | source)
XLA Modules:
  0.0 58.8 jit_solution(16546609673667997862)
XLA Ops:
  0.0 58.0 %triangle_updates.1 = bf16[4,512,128]{2,1,0:T(8,128)(2,1)S(1)} custom-call(bf16[4,512,128]{2,1,0:T(8,128)(2,1)} %x_hbm.1, s32[4,512]{1,0:T(4,128)} %mask_hbm.1, s32[512]{0:T(512)} %chain_hbm.1, f32[2,128]{1,0:T(2,128)} %embed_hbm.1, f32[2,128]{1,0:T(2,128)} %in_gain_hbm.1, f32[2,128]{1,0:T(2,128)} %in_bias_hbm.1, bf16[2,128,256]{2,1,0:T(8,128)(2,1)} %left_hbm.1, ...), custom_call_target="tpu_custom_call" | custom-call | tf_op jit(solution)/shard_map/triangle_updates/pallas_call | solution.py:435
  58.0 0.8 %copy.14 = bf16[4,512,128]{2,1,0:T(8,128)(2,1)} copy(bf16[4,512,128]{2,1,0:T(8,128)(2,1)S(1)} %triangle_updates.1) | data formatting | bytes 1048576

commit v6 on v5

--- a/solution.py
+++ b/solution.py
@@ -12,8 +12,7 @@
 NN, NT = ((1,), (0,)), ((1,), (1,))
 LEFT, RIGHT = 0, 1
 MOVES = (
-    ("right0", 0, 2),
-    ("right0", 2, 2),
+    ("right0", 0, 4),
     ("left0", 0, 4),
     ("left0", 4, 4),
     ("prod0", 0, 2),
@@ -106,6 +105,16 @@
         "prod1": (prod1_send, prod1_recv),
     }
 
+    barrier = pltpu.get_barrier_semaphore()
+
+    def greet(step, carry):
+        pl.semaphore_signal(
+            barrier, inc=1, device_id=lax.rem(me + step, devices), device_id_type=LOGICAL
+        )
+        return carry
+
+    lax.fori_loop(1, devices, greet, 0, unroll=UNROLL)
+
     loads = {}
 
     def fetch(name, source, target):
@@ -129,16 +138,6 @@
     fetch("out_gain", out_gain_hbm, out_gain_ref)
     fetch("out_bias", out_bias_hbm, out_bias_ref)
     fetch("out_w", out_w_hbm, out_w_ref)
-
-    barrier = pltpu.get_barrier_semaphore()
-
-    def greet(step, carry):
-        pl.semaphore_signal(
-            barrier, inc=1, device_id=lax.rem(me + step, devices), device_id_type=LOGICAL
-        )
-        return carry
-
-    lax.fori_loop(1, devices, greet, 0, unroll=UNROLL)
 
     eye = (
         lax.broadcasted_iota(jnp.int32, (LANES, LANES), 0)
@@ -204,21 +203,22 @@
 
     def edges_of_pair(pair, spots):
         span = slice(spots[0] * LANES, (spots[-1] + 1) * LANES)
-        for r in range(2):
-            row = 2 * pair + r
-            mask = mask_ref[row : row + 1, span].astype(F32)
-            normed = layer_norm(
-                state[row, :, span], wide(cols[4], len(spots)), wide(cols[5], len(spots))
-            )
-            normed_rows[row, :, span] = normed
-            for side in (LEFT, RIGHT):
-                value = edge(1, side, normed, mask)
-                for k, cb in enumerate(spots):
-                    low = cb * 2 * LANES
-                    spread[2 + side, pl.ds(low + r, LANES, stride=2), :] = value[:, lanes(k)]
+        count = len(spots)
+        own = (2 * pair, 2 * pair + 1)
+        values = jnp.concatenate([state[row, :, span] for row in own], axis=1)
+        mask = jnp.concatenate([mask_ref[row : row + 1, span] for row in own], axis=1)
+        mask = mask.astype(F32)
+        normed = layer_norm(values, wide(cols[4], 2 * count), wide(cols[5], 2 * count))
+        for r, row in enumerate(own):
+            normed_rows[row, :, span] = normed[:, r * count * LANES : (r + 1) * count * LANES]
         for side in (LEFT, RIGHT):
-            for cb in spots:
+            value = edge(1, side, normed, mask)
+            for k, cb in enumerate(spots):
                 low = cb * 2 * LANES
+                for r in range(2):
+                    spread[2 + side, pl.ds(low + r, LANES, stride=2), :] = value[
+                        :, lanes(r * count + k)
+                    ]
                 edge1_send.at[SLOT[side][pair][cb]].reshape(LANES * 2, LANES)[...] = spread[
                     2 + side, low : low + 2 * LANES, :
                 ].astype(BF16)
@@ -239,15 +239,21 @@
             spread[0, low : low + 2 * LANES, :] = (
                 prod0_recv.at[pair * blocks + jb].reshape(LANES * 2, LANES)[...].astype(F32)
             )
-        for r in range(2):
-            row = 2 * pair + r
-            product = jnp.concatenate(
-                [spread[0, pl.ds(jb * 2 * LANES + r, LANES, stride=2), :] for jb in spots],
-                axis=1,
-            )
-            state[row, :, span] = updated(
-                0, product, state[row, :, span], gating[row, :, span]
-            ).astype(F32)
+        own = (2 * pair, 2 * pair + 1)
+        product = jnp.concatenate(
+            [
+                spread[0, pl.ds(jb * 2 * LANES + r, LANES, stride=2), :]
+                for r in range(2)
+                for jb in spots
+            ],
+            axis=1,
+        )
+        values = jnp.concatenate([state[row, :, span] for row in own], axis=1)
+        gate = jnp.concatenate([gating[row, :, span] for row in own], axis=1)
+        new = updated(0, product, values, gate).astype(F32)
+        width = len(spots) * LANES
+        for r, row in enumerate(own):
+            state[row, :, span] = new[:, r * width : (r + 1) * width]
 
     def finish_columns(cb):
         spread[0, : LANES * rows, :] = (
@@ -312,12 +318,10 @@
     for cb in range(blocks):
         load(cb)
         edges_of_columns(cb)
-        if cb == 1:
-            pl.semaphore_wait(barrier, devices - 1)
-            send_all(0)
+    pl.semaphore_wait(barrier, devices - 1)
+    send_all(0)
     send_all(1)
     send_all(2)
-    send_all(3)
     for row in range(rows):
         gates(0, row)
     fetched("out_gain", "out_bias", "out_w")
@@ -351,13 +355,12 @@
 
     receive(0)
     receive(1)
+    products_of_pair(0, 3)
+    products_of_pair(0, 4)
     receive(2)
-    products_of_pair(0, 4)
-    products_of_pair(0, 5)
-    receive(3)
-    products_of_pair(1, 6)
-
-    for move, pair, then in ((4, 0, (7,)), (5, 0, (8,)), (6, 1, (9, 10))):
+    products_of_pair(1, 5)
+
+    for move, pair, then in ((3, 0, (6,)), (4, 0, (7,)), (5, 1, (8, 9))):
         spots = tuple(slot - pair * blocks for slot in spots_of(move))
         receive(move)
         finish_pair(pair, spots)
@@ -367,7 +370,7 @@
     for row in range(rows):
         gates(1, row)
 
-    for move in (7, 8, 9):
+    for move in (6, 7, 8):
         receive(move)
         for pair in range(pairs):
             for cb in range(blocks):
@@ -376,9 +379,9 @@
                         edge1_recv.at[SLOT[LEFT][pair][cb]].reshape(half, LANES)[...]
                     )
     arrived = 12
-    for move in range(11, len(MOVES)):
+    for move in range(10, len(MOVES)):
         for jb in spots_of(move):
-            for last in (10,):
+            for last in (9,):
                 if SLOT[RIGHT][0][jb] in spots_of(last) and arrived <= SLOT[RIGHT][1][jb]:
                     receive(last)
                     arrived = spots_of(last)[-1] + 1
@@ -391,7 +394,7 @@
             )
             prod1_send.at[jb].reshape(plane, LANES)[...] = dot(left_t[...], right, NN).astype(BF16)
         send_all(move)
-    for move in range(11, len(MOVES)):
+    for move in range(10, len(MOVES)):
         receive(move)
         for cb in spots_of(move):
             finish_columns(cb)

time: 58.9 us -> 58.9 us (level)
  no operation moved by 1% of the time
where the time goes in v6:
time: 58.9 us; the launch traced here: 58.8 us
  Pallas kernels  58 us (98%)
  local copies, waits for them, and re-layouts  0.8 us (1%)
    pallas_call x1, Pallas kernels, shards(): pl.pallas_call(body, out_shape=jax.ShapeDtypeStruct((rows, columns, chan)...  58 us

profile of v6, /device:TPU:1, one launch (start us, length us, event | category | flops | bytes accessed | tf_op | source)
XLA Modules:
  0.0 58.8 jit_solution(1900350478786875845)
XLA Ops:
  0.0 58.0 %triangle_updates.1 = bf16[4,512,128]{2,1,0:T(8,128)(2,1)S(1)} custom-call(bf16[4,512,128]{2,1,0:T(8,128)(2,1)} %x_hbm.1, s32[4,512]{1,0:T(4,128)} %mask_hbm.1, s32[512]{0:T(512)} %chain_hbm.1, f32[2,128]{1,0:T(2,128)} %embed_hbm.1, f32[2,128]{1,0:T(2,128)} %in_gain_hbm.1, f32[2,128]{1,0:T(2,128)} %in_bias_hbm.1, bf16[2,128,256]{2,1,0:T(8,128)(2,1)} %left_hbm.1, ...), custom_call_target="tpu_custom_call" | custom-call | tf_op jit(solution)/shard_map/triangle_updates/pallas_call | solution.py:438
  58.0 0.8 %copy.14 = bf16[4,512,128]{2,1,0:T(8,128)(2,1)} copy(bf16[4,512,128]{2,1,0:T(8,128)(2,1)S(1)} %triangle_updates.1) | data formatting | bytes 1048576
